TPU v7x, 512 devices: a whole 4x8x8 slice. The times are simulated.
512 devices in a mesh: cell: 2 (over core), grp: 256 (over z, y, x).
Axes of the slice: x: 4, y: 8, z: 8, core: 2. Of those that a mesh axis runs over, the one named last changes fastest.
Arguments:
- v_free: float32 [3, 4194304], P(None, 'grp'), may hold values from -6 to 6
- inv_mass: float32 [4194304], P('grp'), may hold values from 0.2 to 5
- pairs: int32 [2, 16384, 128], P(None, ('cell', 'grp')), may hold values from 0 to 20479, as said below
- angles: float32 [2, 16384, 128], P(None, ('cell', 'grp')), may hold values from -3.140625 to 3.140625
- bias: float32 [16384, 128], P(('cell', 'grp')), may hold values from -6 to 6
- friction: float32 [16384, 128], P(('cell', 'grp')), may hold values from 0.2 to 1
- counts: int32 [16384], P(('cell', 'grp')), may hold values from 16 to 128, as said below
Outputs:
- velocity: float32 [3, 4194304], P(None, 'grp')
- impulses: float32 [3, 16384, 128], P(None, ('cell', 'grp'))
Inputs may be any that keep to these rules, and one draw needn't show every extreme that they name: A spatial cell's window of bodies holds the last 2048 bodies of the previous cell (positions 0 to 2047), the cell's own 16384 bodies (positions 2048 to 18431) and the first 2048 bodies of the next cell (the remaining positions). pairs[0] is always one of the cell's own bodies; pairs[1] is another own body or a rim body of a neighbouring cell. No slot of the first cell names the previous rim and no slot of the last cell names the next rim. `counts`: the first block of each 32 blocks is full.
All inputs are finite; a program needn't handle non-finite values.
Results may differ from a plain program's by a relative error of at most 0.0001.
Values sent between devices are 32-bit elements; how exact they have to be, the bound alone decides.
No kernel may reach another device: no remote copies, remote signals or barrier semaphores. Data moves between devices by JAX's collectives and lax.ppermute only.
A program may use at most 128 MiB of HBM per device.

v0:
```python
import jax
import jax.numpy as jnp
from jax import lax
from jax.sharding import PartitionSpec as P

RIM = 2048
ITERS = 3


relax_factor = 0.6
tangent_floor = 0.05


def passed_along(value, axis, steps):
    count = lax.axis_size(axis)
    initial, last = (max(0, -steps), min(count, count - steps))
    return lax.ppermute(value, axis, [(source, source + steps) for source in range(initial, last)])


def extended(block, sides, width):
    for axis, dim in sides:
        count = lax.axis_size(axis)
        forward = [(i, i + 1) for i in range(count - 1)]
        backward = [(target, source) for source, target in forward]
        low = lax.ppermute(
            lax.slice_in_dim(block, block.shape[dim] - width, None, axis=dim), axis, forward
        )
        high = lax.ppermute(lax.slice_in_dim(block, 0, width, axis=dim), axis, backward)
        block = jnp.concatenate([low, block, high], axis=dim)
    return block


def frames(angles):
    sin_polar = jnp.sin(angles[0])
    cos_polar = jnp.cos(angles[0])
    sin_azim = jnp.sin(angles[1])
    cos_azim = jnp.cos(angles[1])
    normal = jnp.stack([sin_polar * cos_azim, sin_polar * sin_azim, cos_polar])
    first_tan = jnp.stack([cos_polar * cos_azim, cos_polar * sin_azim, -sin_polar])
    second_tan = jnp.stack([-sin_azim, cos_azim, jnp.zeros_like(sin_azim)])
    return (normal, first_tan, second_tan)


def contact_update(
    relative, lambdas, normal, first_tan, second_tan, reduced, bias, friction, active
):
    speed_n = jnp.sum(normal * relative, axis=0) + bias
    speed_a = jnp.sum(first_tan * relative, axis=0)
    speed_b = jnp.sum(second_tan * relative, axis=0)
    trial_n = lambdas[0] - relax_factor * reduced * speed_n
    trial_a = lambdas[1] - relax_factor * reduced * speed_a
    trial_b = lambdas[2] - relax_factor * reduced * speed_b
    normal_imp = jnp.maximum(trial_n, 0.0)
    tan_size = jnp.sqrt(trial_a * trial_a + trial_b * trial_b)
    factor = jnp.minimum(1.0, friction * normal_imp / jnp.maximum(tan_size, tangent_floor))
    fresh = jnp.stack([normal_imp, trial_a * factor, trial_b * factor]) * active[None]
    force = normal * fresh[0] + first_tan * fresh[1] + second_tan * fresh[2]
    return (fresh, force)


def fold_rims(total, width):
    to_prev = total[:, :RIM]
    to_next = total[:, RIM + width :]
    from_next = passed_along(to_prev, "grp", -1)
    from_prev = passed_along(to_next, "grp", 1)
    owned = total[:, RIM : RIM + width]
    head = owned[:, :RIM] + from_prev
    tail = owned[:, width - RIM :] + from_next
    return jnp.concatenate([head, owned[:, RIM : width - RIM], tail], axis=1)


def on_device(v_free, inv_mass, pairs, angles, bias, friction, counts):
    width = v_free.shape[1]
    first_pos = pairs[0]
    second_pos = pairs[1]
    slots = jnp.arange(bias.shape[1], dtype=jnp.int32)
    active = (slots[None, :] < counts[:, None]).astype(jnp.float32)
    normal, first_tan, second_tan = frames(angles)
    stacked = jnp.concatenate([v_free, inv_mass[None, :]], axis=0)
    padded = extended(stacked, (("grp", 1),), RIM)
    mass_padded = padded[3]
    vel_padded = padded[:3]
    reduced = 1.0 / (mass_padded[first_pos] + mass_padded[second_pos])
    lambdas = jnp.zeros((3,) + bias.shape, jnp.float32)
    velocity = v_free
    for sweep in range(ITERS):
        if sweep > 0:
            vel_padded = extended(velocity, (("grp", 1),), RIM)
        relative = vel_padded[:, first_pos] - vel_padded[:, second_pos]
        lambdas, force = contact_update(
            relative, lambdas, normal, first_tan, second_tan, reduced, bias, friction, active
        )
        total = jnp.zeros((3, width + 2 * RIM), jnp.float32)
        total = total.at[:, first_pos].add(force).at[:, second_pos].add(-force)
        total = lax.psum(total, "cell")
        owned = fold_rims(total, width)
        velocity = v_free + inv_mass[None, :] * owned
    return (velocity, lambdas)


def solution(mesh):
    return jax.shard_map(
        on_device,
        mesh=mesh,
        in_specs=(
            P(None, "grp"),
            P("grp"),
            P(None, ("cell", "grp"), None),
            P(None, ("cell", "grp"), None),
            P(("cell", "grp"), None),
            P(("cell", "grp"), None),
            P(("cell", "grp")),
        ),
        out_specs=(P(None, "grp"), P(None, ("cell", "grp"), None)),
        check_vma=False,
    )
```

profile of v0, /device:TPU:62, one launch (start us, length us, event | category | flops | bytes accessed | tf_op | source)
XLA Modules:
  0.0 670.0 jit_solution(13365136491902057259)
XLA Ops:
  17.2 4.3 collective-permute-done.1
  22.6 23.0 %gather_fusion.1 = f32[4096]{0:T(1024)S(1)} fusion(f32[20480]{0:T(1024)S(1)} %bitcast.197, s32[4096]{0:T(1024)S(1)} %get-tuple-element.66), kind=kCustom, calls=%fused_computation.1 | custom fusion | bytes 49152 | tf_op jit(solution)/shard_map/gather | solution.py:83
  45.7 23.0 %gather_fusion = f32[4096]{0:T(1024)S(1)} fusion(f32[20480]{0:T(1024)S(1)} %bitcast.198, s32[4096]{0:T(1024)S(1)} %get-tuple-element.67), kind=kCustom, calls=%fused_computation | custom fusion | bytes 49152 | tf_op jit(solution)/shard_map/gather | solution.py:83
  68.9 5.5 copy.85
  74.4 18.2 %gather_fusion.3 = f32[4096,3]{1,0:T(8,128)} fusion(f32[3,20480]{0,1:T(8,128)} %copy.85, s32[4096]{0:T(1024)S(1)} %get-tuple-element.66), kind=kCustom, calls=%fused_computation.3 | custom fusion | bytes 114688 | tf_op jit(solution)/shard_map/gather | solution.py:89
  92.6 18.2 %gather_fusion.2 = f32[4096,3]{1,0:T(8,128)} fusion(f32[3,20480]{0,1:T(8,128)} %copy.85, s32[4096]{0:T(1024)S(1)} %get-tuple-element.67), kind=kCustom, calls=%fused_computation.2 | custom fusion | bytes 114688 | tf_op jit(solution)/shard_map/gather | solution.py:89
  117.4 27.1 %scatter_custom_fusion = f32[3,20480]{0,1:T(8,128)} fusion(s32[4096]{0:T(1024)S(1)} %get-tuple-element.57, f32[4096,3]{1,0:T(8,128)} %bitcast.209, f32[]{:T(128)} %constant.6.clone.1), kind=kCustom, calls=%fused_computation.18 | custom fusion | flops 12288 | bytes 246272 | tf_op jit(solution)/shard_map/scatter-add | solution.py:94
  144.5 27.9 %scatter_fusion = f32[3,20480]{0,1:T(8,128)} fusion(f32[3,20480]{0,1:T(8,128)} %scatter_custom_fusion, s32[4096]{0:T(1024)S(1)} %get-tuple-element.56, f32[4096,3]{1,0:T(8,128)S(1)} %bitcast.206), kind=kCustom, calls=%fused_computation.9 | custom fusion | flops 12288 | bytes 163840 | tf_op jit(solution)/shard_map/scatter-add | solution.py:94
  172.5 61.4 %all-reduce.4.cloned.1.call-done = f32[3,20480]{0,1:T(8,128)} async-done(((f32[3,20480]{0,1:T(8,128)}), f32[3,20480]{0,1:T(8,128)}) %all-reduce.4.cloned.1.call-update) | async-done | bytes 245776 | tf_op jit(solution)/shard_map/psum | solution.py:95
  243.2 7.3 %collective-permute-start.2 = (f32[3,2048]{1,0:T(4,128)}, f32[3,2048]{1,0:T(4,128)S(1)}, u32[]{:S(2)}, u32[]{:S(2)}) collective-permute-start(f32[3,2048]{1,0:T(4,128)} %copy.54), channel_id=1, source_target_pairs={{0,1},{1,2},{2,3},{3,4},{4,5},{5,6},{6,7},{7,8},{8,9},{9,10},{10,1... | collective-permute-start | bytes 73736 | tf_op jit(solution)/shard_map/ppermute | solution.py:17
  250.5 4.7 slice.185
  255.2 4.4 copy.58
  267.3 5.9 collective-permute-done.5
  273.3 5.5 copy.59
  278.9 18.3 %gather_fusion.5 = f32[4096,3]{1,0:T(8,128)} fusion(f32[3,20480]{0,1:T(8,128)} %copy.59, s32[4096]{0:T(1024)S(1)} %copy-done.35), kind=kCustom, calls=%fused_computation.5 | custom fusion | bytes 114688 | tf_op jit(solution)/shard_map/gather | solution.py:89
  297.2 18.2 %gather_fusion.4 = f32[4096,3]{1,0:T(8,128)} fusion(f32[3,20480]{0,1:T(8,128)} %copy.59, s32[4096]{0:T(1024)S(1)} %copy-done.32), kind=kCustom, calls=%fused_computation.4 | custom fusion | bytes 114688 | tf_op jit(solution)/shard_map/gather | solution.py:89
  321.5 27.1 %scatter_custom_fusion.2 = f32[3,20480]{0,1:T(8,128)} fusion(s32[4096]{0:T(1024)} %copy-done.50, f32[4096,3]{1,0:T(8,128)} %bitcast.210, f32[]{:T(128)} %constant.6.clone.1), kind=kCustom, calls=%fused_computation.16 | custom fusion | flops 12288 | bytes 246272 | tf_op jit(solution)/shard_map/scatter-add | solution.py:94
  348.6 27.9 %scatter_fusion.1 = f32[3,20480]{0,1:T(8,128)} fusion(f32[3,20480]{0,1:T(8,128)} %scatter_custom_fusion.2, s32[4096]{0:T(1024)S(1)} %copy-done.44, f32[4096,3]{1,0:T(8,128)S(1)} %bitcast.207), kind=kCustom, calls=%fused_computation.11 | custom fusion | flops 12288 | bytes 163840 | tf_op jit(solution)/shard_map/scatter-add | solution.py:94
  376.6 58.1 %all-reduce.6.cloned.1.call-done = f32[3,20480]{0,1:T(8,128)} async-done(((f32[3,20480]{0,1:T(8,128)}), f32[3,20480]{0,1:T(8,128)}) %all-reduce.6.cloned.1.call-update) | async-done | bytes 245776 | tf_op jit(solution)/shard_map/psum | solution.py:95
  444.0 7.3 %collective-permute-start.6 = (f32[3,2048]{1,0:T(4,128)}, f32[3,2048]{1,0:T(4,128)S(1)}, u32[]{:S(2)}, u32[]{:S(2)}) collective-permute-start(f32[3,2048]{1,0:T(4,128)} %copy.64), channel_id=1, source_target_pairs={{0,1},{1,2},{2,3},{3,4},{4,5},{5,6},{6,7},{7,8},{8,9},{9,10},{10,1... | collective-permute-start | bytes 73736 | tf_op jit(solution)/shard_map/ppermute | solution.py:17
  451.3 4.7 slice.195
  456.1 4.4 copy.68
  468.2 5.9 collective-permute-done.9
  474.2 5.5 copy.69
  479.7 18.2 %gather_fusion.7 = f32[4096,3]{1,0:T(8,128)} fusion(f32[3,20480]{0,1:T(8,128)} %copy.69, s32[4096]{0:T(1024)S(1)} %copy-done.36), kind=kCustom, calls=%fused_computation.7 | custom fusion | bytes 114688 | tf_op jit(solution)/shard_map/gather | solution.py:89
  498.0 18.2 %gather_fusion.6 = f32[4096,3]{1,0:T(8,128)} fusion(f32[3,20480]{0,1:T(8,128)} %copy.69, s32[4096]{0:T(1024)S(1)} %copy-done.33), kind=kCustom, calls=%fused_computation.6 | custom fusion | bytes 114688 | tf_op jit(solution)/shard_map/gather | solution.py:89
  522.2 27.1 %scatter_custom_fusion.4 = f32[3,20480]{0,1:T(8,128)} fusion(s32[4096]{0:T(1024)} %copy-done.50, f32[4096,3]{1,0:T(8,128)} %bitcast.208, f32[]{:T(128)} %constant.6.clone.1), kind=kCustom, calls=%fused_computation.14 | custom fusion | flops 12288 | bytes 246272 | tf_op jit(solution)/shard_map/scatter-add | solution.py:94
  549.3 27.9 %scatter_fusion.2 = f32[3,20480]{0,1:T(8,128)} fusion(f32[3,20480]{0,1:T(8,128)} %scatter_custom_fusion.4, s32[4096]{0:T(1024)S(1)} %copy-done.45, f32[4096,3]{1,0:T(8,128)S(1)} %bitcast.205), kind=kCustom, calls=%fused_computation.13 | custom fusion | flops 12288 | bytes 163840 | tf_op jit(solution)/shard_map/scatter-add | solution.py:94
  577.3 58.2 %all-reduce.8.cloned.1.call-done = f32[3,20480]{0,1:T(8,128)} async-done(((f32[3,20480]{0,1:T(8,128)}), f32[3,20480]{0,1:T(8,128)}) %all-reduce.8.cloned.1.call-update) | async-done | bytes 245776 | tf_op jit(solution)/shard_map/psum | solution.py:95
  644.8 7.3 %collective-permute-start.10 = (f32[3,2048]{1,0:T(4,128)}, f32[3,2048]{1,0:T(4,128)S(1)}, u32[]{:S(2)}, u32[]{:S(2)}) collective-permute-start(f32[3,2048]{1,0:T(4,128)} %copy.74), channel_id=1, source_target_pairs={{0,1},{1,2},{2,3},{3,4},{4,5},{5,6},{6,7},{7,8},{8,9},{9,10},{10,1... | collective-permute-start | bytes 73736 | tf_op jit(solution)/shard_map/ppermute | solution.py:17
  652.0 4.7 slice.205
  656.8 4.4 copy.78
  (192 shorter events, 75.4 us)
Async XLA Ops:
  7.2 226.7 %all-reduce.4.cloned.1.call-start = ((), (), s32[]{:S(2)}) async-start(), calls=%async_computation | async-start | bytes 20971520 | tf_op jit(solution)/shard_map/psum | solution.py:95
  8.1 9.2 %collective-permute-start = (f32[4,2048]{1,0:T(4,128)S(1)}, f32[4,2048]{1,0:T(4,128)S(1)}, u32[]{:S(2)}, u32[]{:S(2)}) collective-permute-start(f32[4,2048]{1,0:T(4,128)S(1)} %get-tuple-element.39), channel_id=1, source_target_pairs={{0,1},{1,2},{2,3},{3,4},{4,5},{5,6},{6,7},{7,8},{8,9},{9,10},{10,1... | collective-permute-start | bytes 98312 | tf_op jit(solution)/shard_map/ppermute | solution.py:25
  11.5 10.0 %collective-permute-start.1 = (f32[4,2048]{1,0:T(4,128)S(1)}, f32[4,2048]{1,0:T(4,128)S(1)}, u32[]{:S(2)}, u32[]{:S(2)}) collective-permute-start(f32[4,2048]{1,0:T(4,128)S(1)} %get-tuple-element.40), channel_id=1, source_target_pairs={{1,0},{2,1},{3,2},{4,3},{5,4},{6,5},{7,6},{8,7},{9,8},{10,9},{11,1... | collective-permute-start | bytes 98312 | tf_op jit(solution)/shard_map/ppermute | solution.py:28
  14.7 102.7 %copy-start.50 = (s32[4096]{0:T(1024)}, s32[4096]{0:T(1024)S(1)}, u32[]{:S(2)}) copy-start(s32[4096]{0:T(1024)S(1)} %get-tuple-element.57) | copy-start | bytes 49156
  14.7 129.9 %copy-start.43 = (s32[4096]{0:T(1024)}, s32[4096]{0:T(1024)S(1)}, u32[]{:S(2)}) copy-start(s32[4096]{0:T(1024)S(1)} %get-tuple-element.56) | copy-start | bytes 49156
  15.4 58.9 %copy-start.34 = (s32[4096]{0:T(1024)}, s32[4096]{0:T(1024)S(1)}, u32[]{:S(2)}) copy-start(s32[4096]{0:T(1024)S(1)} %get-tuple-element.66) | copy-start | bytes 49156
  15.4 77.1 %copy-start.31 = (s32[4096]{0:T(1024)}, s32[4096]{0:T(1024)S(1)}, u32[]{:S(2)}) copy-start(s32[4096]{0:T(1024)S(1)} %get-tuple-element.67) | copy-start | bytes 49156
  16.3 98.2 %copy-start.2 = (f32[1,32,128]{2,1,0:T(8,128)}, f32[1,32,128]{2,1,0:T(8,128)S(1)}, u32[]{:S(2)}) copy-start(f32[1,32,128]{2,1,0:T(8,128)S(1)} %get-tuple-element.58) | copy-start | bytes 49156
  16.3 98.2 %copy-start.4 = (f32[1,32,128]{2,1,0:T(8,128)}, f32[1,32,128]{2,1,0:T(8,128)S(1)}, u32[]{:S(2)}) copy-start(f32[1,32,128]{2,1,0:T(8,128)S(1)} %get-tuple-element.59) | copy-start | bytes 49156
  16.3 98.2 %copy-start.6 = (f32[1,32,128]{2,1,0:T(8,128)}, f32[1,32,128]{2,1,0:T(8,128)S(1)}, u32[]{:S(2)}) copy-start(f32[1,32,128]{2,1,0:T(8,128)S(1)} %get-tuple-element.60) | copy-start | bytes 49156
  16.4 98.2 %copy-start.8 = (f32[1,32,128]{2,1,0:T(8,128)}, f32[1,32,128]{2,1,0:T(8,128)S(1)}, u32[]{:S(2)}) copy-start(f32[1,32,128]{2,1,0:T(8,128)S(1)} %get-tuple-element.61) | copy-start | bytes 49156
  16.4 98.2 %copy-start.10 = (f32[1,32,128]{2,1,0:T(8,128)}, f32[1,32,128]{2,1,0:T(8,128)S(1)}, u32[]{:S(2)}) copy-start(f32[1,32,128]{2,1,0:T(8,128)S(1)} %get-tuple-element.62) | copy-start | bytes 49156
  16.4 98.2 %copy-start.12 = (f32[1,32,128]{2,1,0:T(8,128)}, f32[1,32,128]{2,1,0:T(8,128)S(1)}, u32[]{:S(2)}) copy-start(f32[1,32,128]{2,1,0:T(8,128)S(1)} %get-tuple-element.63) | copy-start | bytes 49156
  16.4 98.2 %copy-start.15 = (f32[1,32,128]{2,1,0:T(8,128)}, f32[1,32,128]{2,1,0:T(8,128)S(1)}, u32[]{:S(2)}) copy-start(f32[1,32,128]{2,1,0:T(8,128)S(1)} %get-tuple-element.64) | copy-start | bytes 49156
  16.4 98.2 %copy-start.18 = (f32[1,32,128]{2,1,0:T(8,128)}, f32[1,32,128]{2,1,0:T(8,128)S(1)}, u32[]{:S(2)}) copy-start(f32[1,32,128]{2,1,0:T(8,128)S(1)} %get-tuple-element.65) | copy-start | bytes 49156
  17.1 97.4 %copy-start.37 = (f32[32,128]{1,0:T(8,128)}, f32[32,128]{1,0:T(8,128)S(1)}, u32[]{:S(2)}) copy-start(f32[32,128]{1,0:T(8,128)S(1)} %fusion.32) | copy-start | bytes 49156
  17.2 97.4 %copy-start.47 = (f32[3]{0:T(128)}, f32[3]{0:T(128)S(1)}, u32[]{:S(2)}) copy-start(f32[3]{0:T(128)S(1)} %pad.26.clone) | copy-start | bytes 40
  172.5 262.3 %all-reduce.6.cloned.1.call-start = ((), (), s32[]{:S(2)}) async-start(), calls=%async_computation.1 | async-start | bytes 20971520 | tf_op jit(solution)/shard_map/psum | solution.py:95
  239.5 20.8 %collective-permute-start.3 = (f32[3,2048]{1,0:T(4,128)}, f32[3,2048]{1,0:T(4,128)}, u32[]{:S(2)}, u32[]{:S(2)}) collective-permute-start(f32[3,2048]{1,0:T(4,128)} %copy.56), channel_id=1, source_target_pairs={{1,0},{2,1},{3,2},{4,3},{5,4},{6,5},{7,6},{8,7},{9,8},{10,9},{11,1... | collective-permute-start | bytes 73736 | tf_op jit(solution)/shard_map/ppermute | solution.py:17
  243.2 17.9 %collective-permute-start.2 = (f32[3,2048]{1,0:T(4,128)}, f32[3,2048]{1,0:T(4,128)S(1)}, u32[]{:S(2)}, u32[]{:S(2)}) collective-permute-start(f32[3,2048]{1,0:T(4,128)} %copy.54), channel_id=1, source_target_pairs={{0,1},{1,2},{2,3},{3,4},{4,5},{5,6},{6,7},{7,8},{8,9},{9,10},{10,1... | collective-permute-start | bytes 73736 | tf_op jit(solution)/shard_map/ppermute | solution.py:17
  261.3 6.0 collective-permute-start.4
  263.2 10.0 %collective-permute-start.5 = (f32[3,2048]{1,0:T(4,128)S(1)}, f32[3,2048]{1,0:T(4,128)S(1)}, u32[]{:S(2)}, u32[]{:S(2)}) collective-permute-start(f32[3,2048]{1,0:T(4,128)S(1)} %get-tuple-element.44), channel_id=1, source_target_pairs={{1,0},{2,1},{3,2},{4,3},{5,4},{6,5},{7,6},{8,7},{9,8},{10,9},{11,1... | collective-permute-start | bytes 73736 | tf_op jit(solution)/shard_map/ppermute | solution.py:28
  278.9 39.7 %copy-start.24 = (f32[3,32,128]{2,1,0:T(8,128)S(1)}, f32[3,32,128]{2,1,0:T(8,128)}, u32[]{:S(2)}) copy-start(f32[3,32,128]{2,1,0:T(8,128)} %copy-done.23) | copy-start | bytes 147460
  278.9 39.7 %copy-start.26 = (f32[4096]{0:T(1024)S(1)}, f32[4096]{0:T(1024)}, u32[]{:S(2)}) copy-start(f32[4096]{0:T(1024)} %copy-done.25) | copy-start | bytes 49156
  278.9 39.8 %copy-start.38 = (f32[32,128]{1,0:T(8,128)S(1)}, f32[32,128]{1,0:T(8,128)}, u32[]{:S(2)}) copy-start(f32[32,128]{1,0:T(8,128)} %copy-done.37) | copy-start | bytes 49156
  376.6 258.9 %all-reduce.8.cloned.1.call-start = ((), (), s32[]{:S(2)}) async-start(), calls=%async_computation.2 | async-start | bytes 20971520 | tf_op jit(solution)/shard_map/psum | solution.py:95
  440.3 20.8 %collective-permute-start.7 = (f32[3,2048]{1,0:T(4,128)}, f32[3,2048]{1,0:T(4,128)}, u32[]{:S(2)}, u32[]{:S(2)}) collective-permute-start(f32[3,2048]{1,0:T(4,128)} %copy.66), channel_id=1, source_target_pairs={{1,0},{2,1},{3,2},{4,3},{5,4},{6,5},{7,6},{8,7},{9,8},{10,9},{11,1... | collective-permute-start | bytes 73736 | tf_op jit(solution)/shard_map/ppermute | solution.py:17
  444.0 17.9 %collective-permute-start.6 = (f32[3,2048]{1,0:T(4,128)}, f32[3,2048]{1,0:T(4,128)S(1)}, u32[]{:S(2)}, u32[]{:S(2)}) collective-permute-start(f32[3,2048]{1,0:T(4,128)} %copy.64), channel_id=1, source_target_pairs={{0,1},{1,2},{2,3},{3,4},{4,5},{5,6},{6,7},{7,8},{8,9},{9,10},{10,1... | collective-permute-start | bytes 73736 | tf_op jit(solution)/shard_map/ppermute | solution.py:17
  462.1 6.1 collective-permute-start.8
  464.1 10.0 %collective-permute-start.9 = (f32[3,2048]{1,0:T(4,128)S(1)}, f32[3,2048]{1,0:T(4,128)S(1)}, u32[]{:S(2)}, u32[]{:S(2)}) collective-permute-start(f32[3,2048]{1,0:T(4,128)S(1)} %get-tuple-element.42), channel_id=1, source_target_pairs={{1,0},{2,1},{3,2},{4,3},{5,4},{6,5},{7,6},{8,7},{9,8},{10,9},{11,1... | collective-permute-start | bytes 73736 | tf_op jit(solution)/shard_map/ppermute | solution.py:28
  641.1 20.8 %collective-permute-start.11 = (f32[3,2048]{1,0:T(4,128)}, f32[3,2048]{1,0:T(4,128)}, u32[]{:S(2)}, u32[]{:S(2)}) collective-permute-start(f32[3,2048]{1,0:T(4,128)} %copy.76), channel_id=1, source_target_pairs={{1,0},{2,1},{3,2},{4,3},{5,4},{6,5},{7,6},{8,7},{9,8},{10,9},{11,1... | collective-permute-start | bytes 73736 | tf_op jit(solution)/shard_map/ppermute | solution.py:17
  644.8 17.9 %collective-permute-start.10 = (f32[3,2048]{1,0:T(4,128)}, f32[3,2048]{1,0:T(4,128)S(1)}, u32[]{:S(2)}, u32[]{:S(2)}) collective-permute-start(f32[3,2048]{1,0:T(4,128)} %copy.74), channel_id=1, source_target_pairs={{0,1},{1,2},{2,3},{3,4},{4,5},{5,6},{6,7},{7,8},{8,9},{9,10},{10,1... | collective-permute-start | bytes 73736 | tf_op jit(solution)/shard_map/ppermute | solution.py:17
  (34 other events, 1171.1 us)
Sparse Core Ops, SparseCore 0:
  172.6 61.2 all-reduce.3
  376.7 58.0 all-reduce.5
  577.4 58.0 all-reduce.7
where the time goes:
time: 672 us; the launch traced here: 670 us
  local copies, waits for them, and re-layouts  231 us (34%)
  waiting for transfers between devices  194 us (29%)
  other arithmetic  182 us (27%)
  starting transfers between devices  48.2 us (7%)
  between operations  14.7 us (2%)
    psum x3, waiting for transfers between devices, on_device(): total = lax.psum(total, 'cell')  178 us
    scatter-add x6, other arithmetic, on_device(): total = total.at[:, first_pos].add(force).at[:, second_pos].add(-force)  165 us
    gather x6, local copies, waits for them, and re-layouts, on_device(): relative = vel_padded[:, first_pos] - vel_padded[:, second_pos]  109 us
    gather x2, local copies, waits for them, and re-layouts, on_device(): reduced = 1.0 / (mass_padded[first_pos] + mass_padded[second_pos])  46.1 us
    ppermute x6, starting transfers between devices, passed_along(): lax.ppermute(value, axis, [(source, source + steps) for source in range(i...  30.1 us
    slice x6, local copies, waits for them, and re-layouts, fold_rims(): return jnp.concatenate([head, owned[:, RIM:width - RIM], tail], axis=1)  27.5 us
    ppermute x3, waiting for transfers between devices, extended(): lax.ppermute(lax.slice_in_dim(block, 0, width, axis=dim), axis, backward)  16.1 us
  transfers between devices with their start and end apart: 15, of which 6 were waited for; matrix products, arithmetic and copies ran while one was open for 6% of the time, Pallas kernels for 0%

commit v1 on v0

v1 whole, which is shorter than its diff:
```python
import jax
import jax.numpy as jnp
from jax import lax
from jax.experimental import pallas as pl
from jax.experimental.pallas import tpu as pltpu
from jax.sharding import PartitionSpec as P

RIM = 2048
ITERS = 3
LANES = 128
relax_factor = 0.6
tangent_floor = 0.05

f32 = jnp.float32
bf16 = jnp.bfloat16


def call(body, out_shapes, *args, specs=None, scratch=()):
    kw = {} if specs is None else {"in_specs": specs}
    return pl.pallas_call(
        body,
        out_shape=[jax.ShapeDtypeStruct(s, f32) for s in out_shapes],
        scratch_shapes=list(scratch),
        **kw,
    )(*args)


def gather_rows(table, comps, start, rows, base, positions, sums):
    his = [p // LANES for p in positions]
    los = [p % LANES for p in positions]

    def group(g, sums):
        sums = [list(s) for s in sums]
        first = pl.multiple_of(start + g * 8, 8)
        for j in range(8):
            hits = [hi == first + (base + j) for hi in his]
            for c in range(comps):
                row = jnp.broadcast_to(table[c, pl.ds(first + j, 1), :], los[0].shape)
                for k, lo in enumerate(los):
                    got = jnp.take_along_axis(row, lo, axis=1, mode="promise_in_bounds")
                    sums[k][c] = jnp.where(hits[k], got, sums[k][c])
        return tuple(tuple(s) for s in sums)

    init = tuple(tuple(s) for s in sums)
    return lax.fori_loop(0, rows // 8, group, init)


def update(lam, rel, trig, scaled, bias, friction, active):
    sp, cp, sq, cq = trig
    n = (sp * cq, sp * sq, cp)
    a = (cp * cq, cp * sq, -sp)
    b = (-sq, cq)
    un = (n[0] * rel[0] + n[1] * rel[1] + n[2] * rel[2]) + bias
    ua = a[0] * rel[0] + a[1] * rel[1] + a[2] * rel[2]
    ub = b[0] * rel[0] + b[1] * rel[1]
    yn = lam[0] - scaled * un
    ya = lam[1] - scaled * ua
    yb = lam[2] - scaled * ub
    top = jnp.maximum(yn, 0.0)
    size = jnp.sqrt(ya * ya + yb * yb)
    factor = jnp.minimum(1.0, friction * top / jnp.maximum(size, tangent_floor))
    fn = active * top
    fa = active * (factor * ya)
    fb = active * (factor * yb)
    force = (
        n[0] * fn + a[0] * fa + b[0] * fb,
        n[1] * fn + a[1] * fa + b[1] * fb,
        n[2] * fn + a[2] * fa,
    )
    return (fn, fa, fb), force


def scatter(pairs, force, lhs, rhs, stage, out, rows):
    half = rows // 2
    blocks = pairs.shape[1]
    for c in range(3):
        high = force[c].astype(bf16).astype(f32)
        stage[2 * c] = high
        stage[2 * c + 1] = force[c] - high
    row_ids = lax.broadcasted_iota(jnp.int32, (half, LANES), 0).astype(f32).astype(bf16)
    col_ids = lax.broadcasted_iota(jnp.int32, (2 * LANES, LANES), 0).astype(f32).astype(bf16)
    for side in range(2):
        pos = pairs[side]
        hi = pos // LANES
        upper = (hi >= half).astype(jnp.int32)
        stage[6 + 2 * side] = (hi - half * upper).astype(f32)
        stage[7 + 2 * side] = (pos % LANES + LANES * upper).astype(f32)
    one = jnp.ones((), bf16)
    zero = jnp.zeros((), bf16)

    def wide(k, b, n):
        return jnp.broadcast_to(stage[k, pl.ds(b, 1), :], (n, LANES)).astype(bf16)

    for b in range(blocks):
        vals = [wide(k, b, half) for k in range(6)]
        for side in range(2):
            at = pl.ds((2 * b + side) * LANES, LANES)
            hit = wide(6 + 2 * side, b, half) == row_ids
            for k in range(6):
                lhs[pl.ds(k * half, half), at] = jnp.where(hit, vals[k], zero)
            col = wide(7 + 2 * side, b, 2 * LANES) == col_ids
            rhs[:, at] = jnp.where(col, one if side == 0 else -one, zero)
    prod = lax.dot_general(
        lhs[...], rhs[...], (((1,), (1,)), ((), ())), preferred_element_type=f32
    )
    for c in range(3):
        both = prod[2 * c * half : (2 * c + 1) * half] + prod[(2 * c + 1) * half : (2 * c + 2) * half]
        out[c, :half, :] = both[:, :LANES]
        out[c, half:, :] = both[:, LANES:]


def scatter_scratch(rows, blocks):
    deep = 2 * blocks * LANES
    return (
        pltpu.VMEM((3 * rows, deep), bf16),
        pltpu.VMEM((2 * LANES, deep), bf16),
        pltpu.VMEM((10, blocks, LANES), f32),
    )


def on_device(v_free, inv_mass, pairs, angles, bias, friction, counts):
    width = v_free.shape[1]
    own = width // LANES
    rim = RIM // LANES
    rows = own + 2 * rim
    blocks = bias.shape[0]
    slots = (blocks, LANES)
    count = lax.axis_size("grp")
    up = [(i, i + 1) for i in range(count - 1)]
    down = [(i + 1, i) for i in range(count - 1)]
    partner = [(0, 1), (1, 0)]

    def to_both(low, high):
        return lax.ppermute(high, "grp", up), lax.ppermute(low, "grp", down)

    mass2 = inv_mass.reshape(own, LANES)
    stacked = jnp.concatenate([v_free, inv_mass[None, :]], axis=0)
    from_prev, from_next = to_both(stacked[:, :RIM], stacked[:, width - RIM :])

    def prepare(v_ref, mass_ref, pairs_ref, angles_ref, counts_ref, vf, part, trig, act):
        for r in range(own):
            for c in range(3):
                vf[c, r : r + 1, :] = v_ref[c : c + 1, r * LANES : (r + 1) * LANES]
        vf[3] = mass_ref[...]
        for i in range(2):
            trig[2 * i] = jnp.sin(angles_ref[i])
            trig[2 * i + 1] = jnp.cos(angles_ref[i])
        lane = lax.broadcasted_iota(jnp.int32, (1, LANES), 1)
        for b in range(blocks):
            act[b : b + 1, :] = jnp.where(lane < counts_ref[b], 1.0, 0.0)
        zero = jnp.zeros((8, LANES), f32)
        for k in range(blocks // 8):
            at = slice(8 * k, 8 * k + 8)
            one, two = gather_rows(
                vf, 4, 0, own, rim, [pairs_ref[0, at, :], pairs_ref[1, at, :]], [[zero] * 4, [zero] * 4]
            )
            for c in range(4):
                part[c, at, :] = one[c]
                part[4 + c, at, :] = two[c]

    vmem = pl.BlockSpec(memory_space=pltpu.VMEM)
    smem = pl.BlockSpec(memory_space=pltpu.SMEM)
    vf, part, trig, act = call(
        prepare,
        [(4, own, LANES), (8,) + slots, (4,) + slots, slots],
        v_free, mass2, pairs, angles, counts,
        specs=[vmem] * 4 + [smem],
    )

    def first_sweep(part_ref, prev_ref, next_ref, pairs_ref, trig_ref, act_ref, bias_ref, fric_ref,
                    rims, scaled_ref, lam_ref, total, lhs, rhs, stage):
        for r in range(rim):
            for c in range(4):
                at = slice(r * LANES, (r + 1) * LANES)
                rims[c, r : r + 1, :] = prev_ref[c : c + 1, at]
                rims[c, rim + r : rim + r + 1, :] = next_ref[c : c + 1, at]
        two = [part_ref[4 + c] for c in range(4)]
        pos = pairs_ref[1]
        (two,) = gather_rows(rims, 4, 0, rim, 0, [pos], [two])
        (two,) = gather_rows(rims, 4, rim, rim, own, [pos], [two])
        rel = [part_ref[c] - two[c] for c in range(3)]
        scaled = relax_factor * (1.0 / (part_ref[3] + two[3]))
        scaled_ref[...] = scaled
        zero = jnp.zeros(slots, f32)
        fresh, force = update(
            (zero, zero, zero), rel, [trig_ref[k] for k in range(4)], scaled, bias_ref[...], fric_ref[...], act_ref[...]
        )
        for c in range(3):
            lam_ref[c] = fresh[c]
        scatter(pairs_ref, force, lhs, rhs, stage, total, rows)

    rims, scaled, lam, total = call(
        first_sweep,
        [(4, 2 * rim, LANES), slots, (3,) + slots, (3, rows, LANES)],
        part, from_prev, from_next, pairs, trig, act, bias, friction,
        scratch=scatter_scratch(rows, blocks),
    )

    for sweep in range(1, ITERS):
        other = lax.ppermute(total, "cell", partner)
        edge_low = total[:, : 2 * rim] + other[:, : 2 * rim]
        edge_high = total[:, own:] + other[:, own:]
        got_prev, got_next = to_both(edge_low, edge_high)

        def inner(total_ref, other_ref, vf_ref, pairs_ref, part, vel):
            for c in range(3):
                vel[c] = vf_ref[c, rim : own - rim] + vf_ref[3, rim : own - rim] * (
                    total_ref[c, 2 * rim : own] + other_ref[c, 2 * rim : own]
                )
            zero = jnp.zeros((8, LANES), f32)
            for k in range(blocks // 8):
                at = slice(8 * k, 8 * k + 8)
                one, two = gather_rows(
                    vel, 3, 0, own - 2 * rim, 2 * rim,
                    [pairs_ref[0, at, :], pairs_ref[1, at, :]], [[zero] * 3, [zero] * 3],
                )
                for c in range(3):
                    part[c, at, :] = one[c]
                    part[3 + c, at, :] = two[c]

        (part,) = call(
            inner, [(6,) + slots], total, other, vf, pairs,
            scratch=[pltpu.VMEM((3, own - 2 * rim, LANES), f32)],
        )

        def outer(part_ref, low_ref, high_ref, prev_ref, next_ref, vf_ref, rims_ref, pairs_ref, trig_ref, act_ref,
                  bias_ref, fric_ref, scaled_ref, old_ref, lam_ref, total, vel, lhs, rhs, stage):
            for c in range(3):
                low = low_ref[c] + prev_ref[c]
                high = high_ref[c] + next_ref[c]
                vel[c, :rim] = rims_ref[c, :rim] + rims_ref[3, :rim] * low[:rim]
                vel[c, rim : 2 * rim] = vf_ref[c, :rim] + vf_ref[3, :rim] * low[rim:]
                vel[c, 2 * rim : 3 * rim] = vf_ref[c, own - rim :] + vf_ref[3, own - rim :] * high[:rim]
                vel[c, 3 * rim :] = rims_ref[c, rim:] + rims_ref[3, rim:] * high[rim:]
            for k in range(blocks // 8):
                at = slice(8 * k, 8 * k + 8)
                sums = [[part_ref[c, at, :] for c in range(3)], [part_ref[3 + c, at, :] for c in range(3)]]
                both = [pairs_ref[0, at, :], pairs_ref[1, at, :]]
                sums = gather_rows(vel, 3, 0, 2 * rim, 0, both, sums)
                one, two = gather_rows(vel, 3, 2 * rim, 2 * rim, own - 2 * rim, both, sums)
                rel = [one[c] - two[c] for c in range(3)]
                fresh, force = update(
                    [old_ref[c, at, :] for c in range(3)], rel, [trig_ref[i, at, :] for i in range(4)],
                    scaled_ref[at, :], bias_ref[at, :], fric_ref[at, :], act_ref[at, :],
                )
                for c in range(3):
                    lam_ref[c, at, :] = fresh[c]
                    stage[c, at, :] = force[c]
            scatter(pairs_ref, [stage[c] for c in range(3)], lhs, rhs, stage, total, rows)

        lam, total = call(
            outer,
            [(3,) + slots, (3, rows, LANES)],
            part, edge_low, edge_high, got_prev, got_next, vf, rims, pairs, trig, act, bias, friction, scaled, lam,
            scratch=(pltpu.VMEM((3, 4 * rim, LANES), f32),) + scatter_scratch(rows, blocks),
        )

    other = lax.ppermute(total, "cell", partner)
    low = total[:, : 2 * rim] + other[:, : 2 * rim]
    high = total[:, own:] + other[:, own:]
    got_prev, got_next = to_both(low[:, :rim], high[:, rim:])

    def finish(total_ref, other_ref, prev_ref, next_ref, vf_ref, out):
        for c in range(3):
            t = total_ref[c, rim : rim + own] + other_ref[c, rim : rim + own]
            head = t[:rim] + prev_ref[c]
            tail = t[own - rim :] + next_ref[c]
            v = vf_ref[c] + vf_ref[3] * jnp.concatenate([head, t[rim : own - rim], tail], axis=0)
            for r in range(own):
                out[c : c + 1, r * LANES : (r + 1) * LANES] = v[r : r + 1]

    (velocity,) = call(finish, [(3, width)], total, other, got_prev, got_next, vf)
    return (velocity, lam)


def solution(mesh):
    return jax.shard_map(
        on_device,
        mesh=mesh,
        in_specs=(
            P(None, "grp"),
            P("grp"),
            P(None, ("cell", "grp"), None),
            P(None, ("cell", "grp"), None),
            P(("cell", "grp"), None),
            P(("cell", "grp"), None),
            P(("cell", "grp")),
        ),
        out_specs=(P(None, "grp"), P(None, ("cell", "grp"), None)),
        check_vma=False,
    )
```

time: 672 us -> 116 us (0.17)
  the two profiles are of different devices: /device:TPU:62 before, /device:TPU:256 now
where the time goes in v1:
time: 116 us; the launch traced here: 115 us
  Pallas kernels  52.1 us (45%)
  starting transfers between devices  42.7 us (37%)
  waiting for transfers between devices  13 us (11%)
  local copies, waits for them, and re-layouts  3.32 us (3%)
  other arithmetic  2.68 us (2%)
    pallas_call x7, Pallas kernels, call(): pl.pallas_call(body, out_shape=[jax.ShapeDtypeStruct(s, f32) for s in out...  52.1 us
    ppermute x8, starting transfers between devices, to_both(): return (lax.ppermute(high, 'grp', up), lax.ppermute(low, 'grp', down))  37 us
    ppermute x8, waiting for transfers between devices, to_both(): return (lax.ppermute(high, 'grp', up), lax.ppermute(low, 'grp', down))  8.81 us
    ppermute x3, starting transfers between devices, on_device(): other = lax.ppermute(total, 'cell', partner)  5.72 us
    ppermute x3, waiting for transfers between devices, on_device(): other = lax.ppermute(total, 'cell', partner)  4.23 us
    unnamed x30, local copies, waits for them, and re-layouts  2.47 us
  transfers between devices with their start and end apart: 11, of which 4 were waited for; matrix products, arithmetic and copies ran while one was open for 1% of the time, Pallas kernels for 23%

profile of v1, /device:TPU:256, one launch (start us, length us, event | category | flops | bytes accessed | tf_op | source)
XLA Modules:
  0.0 114.8 jit_solution(7111055193699509951)
XLA Ops:
  0.6 0.8 pad_maximum_fusion
  1.5 6.7 %collective-permute-start.1 = (f32[4,2048]{1,0:T(4,128)S(1)}, f32[4,2048]{1,0:T(4,128)S(1)}, u32[]{:S(2)}, u32[]{:S(2)}) collective-permute-start(f32[4,2048]{1,0:T(4,128)S(1)} %get-tuple-element.30), channel_id=1, source_target_pairs={{1,0},{2,1},{3,2},{4,3},{5,4},{6,5},{7,6},{8,7},{9,8},{10,9},{11,1... | collective-permute-start | bytes 98312 | tf_op jit(solution)/shard_map/ppermute | solution.py:134
  8.1 1.9 %collective-permute-start = (f32[4,2048]{1,0:T(4,128)S(1)}, f32[4,2048]{1,0:T(4,128)S(1)}, u32[]{:S(2)}, u32[]{:S(2)}) collective-permute-start(f32[4,2048]{1,0:T(4,128)S(1)} %get-tuple-element.31), channel_id=1, source_target_pairs={{0,1},{1,2},{2,3},{3,4},{4,5},{5,6},{6,7},{7,8},{8,9},{9,10},{10,1... | collective-permute-start | bytes 98312 | tf_op jit(solution)/shard_map/ppermute | solution.py:134
  10.1 11.0 %shard_map.86 = (f32[4,128,128]{2,1,0:T(8,128)}, f32[8,32,128]{2,1,0:T(8,128)}, f32[4,32,128]{2,1,0:T(8,128)}, f32[32,128]{1,0:T(8,128)}) custom-call(f32[3,16384]{1,0:T(4,128)} %v_ref.1, f32[128,128]{1,0:T(8,128)} %bitcast.3, s32[2,32,128]{2,1,0:T(8,128)} %pairs_ref.11, f32[2,32,128]{2,1,0:T(8,128)} %angles_ref.1, s32[32]{0:T(128)} %counts_ref.1), custom_call_target="tpu_custom_call" | custom-call | tf_op jit(solution)/shard_map/pallas_call | solution.py:20
  21.1 0.6 copy-done.11
  21.7 0.0 copy-done.12
  21.7 6.1 %shard_map.87 = (f32[4,32,128]{2,1,0:T(8,128)}, f32[32,128]{1,0:T(8,128)}, f32[3,32,128]{2,1,0:T(8,128)}, f32[3,160,128]{2,1,0:T(8,128)}) custom-call(f32[8,32,128]{2,1,0:T(8,128)} %get-tuple-element.14.part_ref, f32[4,2048]{1,0:T(4,128)} %copy-done.12, f32[4,2048]{1,0:T(4,128)} %copy-done.11, s32[2,32,128]{2,1,0:T(8,128)} %pairs_ref.11, ...), custom_call_target="tpu_custom_call" | custom-call | tf_op jit(solution)/shard_map/pallas_call | solution.py:20
  27.9 1.9 %collective-permute-start.2 = (f32[3,160,128]{2,1,0:T(8,128)}, f32[3,160,128]{2,1,0:T(8,128)S(1)}, u32[]{:S(2)}, u32[]{:S(2)}) collective-permute-start(f32[3,160,128]{2,1,0:T(8,128)} %get-tuple-element.17.total_ref), channel_id=1, source_target_pairs={{0,256},{256,0},{1,257},{257,1},{2,258},{258,2},{3,259},{259,3},{4... | collective-permute-start | bytes 737288 | tf_op jit(solution)/shard_map/ppermute | solution.py:200
  29.8 1.7 %collective-permute-done.2.other_ref = f32[3,160,128]{2,1,0:T(8,128)S(1)} collective-permute-done((f32[3,160,128]{2,1,0:T(8,128)}, f32[3,160,128]{2,1,0:T(8,128)S(1)}, u32[]{:S(2)}, u32[]{:S(2)}) %collective-permute-start.2) | collective-permute-done | bytes 245792 | tf_op jit(solution)/shard_map/ppermute | solution.py:200
  31.5 0.9 slice_add_fusion.2
  32.4 1.9 %collective-permute-start.3 = (f32[3,32,128]{2,1,0:T(8,128)S(1)}, f32[3,32,128]{2,1,0:T(8,128)S(1)}, u32[]{:S(2)}, u32[]{:S(2)}) collective-permute-start(f32[3,32,128]{2,1,0:T(8,128)S(1)} %get-tuple-element.28.high_ref), channel_id=1, source_target_pairs={{0,1},{1,2},{2,3},{3,4},{4,5},{5,6},{6,7},{7,8},{8,9},{9,10},{10,1... | collective-permute-start | bytes 147464 | tf_op jit(solution)/shard_map/ppermute | solution.py:134
  34.3 9.4 %collective-permute-start.4 = (f32[3,32,128]{2,1,0:T(8,128)S(1)}, f32[3,32,128]{2,1,0:T(8,128)S(1)}, u32[]{:S(2)}, u32[]{:S(2)}) collective-permute-start(f32[3,32,128]{2,1,0:T(8,128)S(1)} %get-tuple-element.29.low_ref), channel_id=1, source_target_pairs={{1,0},{2,1},{3,2},{4,3},{5,4},{6,5},{7,6},{8,7},{9,8},{10,9},{11,1... | collective-permute-start | bytes 147464 | tf_op jit(solution)/shard_map/ppermute | solution.py:134
  43.7 7.8 %shard_map.88.part_ref = f32[6,32,128]{2,1,0:T(8,128)} custom-call(f32[3,160,128]{2,1,0:T(8,128)} %get-tuple-element.17.total_ref, f32[3,160,128]{2,1,0:T(8,128)} %copy-done.1, f32[4,128,128]{2,1,0:T(8,128)} %get-tuple-element.18.vf_ref, s32[2,32,128]{2,1,0:T(8,128)} %pairs_ref.11), custom_call_target="tpu_custom_call" | custom-call | tf_op jit(solution)/shard_map/pallas_call | solution.py:20
  51.6 0.6 copy-done.8
  52.2 0.0 copy-done.10
  52.2 8.6 %shard_map.89 = (f32[3,32,128]{2,1,0:T(8,128)}, f32[3,160,128]{2,1,0:T(8,128)}) custom-call(f32[6,32,128]{2,1,0:T(8,128)} %shard_map.88.part_ref, f32[3,32,128]{2,1,0:T(8,128)} %copy-done.6, f32[3,32,128]{2,1,0:T(8,128)} %copy-done.5, f32[3,32,128]{2,1,0:T(8,128)} %copy-done.8, f32[3,32,128]{2,1,0:T(8,128)} %copy-done.10, ...), custom_call_target="tpu_custom_call" | custom-call | tf_op jit(solution)/shard_map/pallas_call | solution.py:20
  60.8 1.9 %collective-permute-start.5 = (f32[3,160,128]{2,1,0:T(8,128)}, f32[3,160,128]{2,1,0:T(8,128)S(1)}, u32[]{:S(2)}, u32[]{:S(2)}) collective-permute-start(f32[3,160,128]{2,1,0:T(8,128)} %get-tuple-element.22.total_ref), channel_id=1, source_target_pairs={{0,256},{256,0},{1,257},{257,1},{2,258},{258,2},{3,259},{259,3},{4... | collective-permute-start | bytes 737288 | tf_op jit(solution)/shard_map/ppermute | solution.py:200
  62.7 1.7 %collective-permute-done.5.other_ref = f32[3,160,128]{2,1,0:T(8,128)S(1)} collective-permute-done((f32[3,160,128]{2,1,0:T(8,128)}, f32[3,160,128]{2,1,0:T(8,128)S(1)}, u32[]{:S(2)}, u32[]{:S(2)}) %collective-permute-start.5) | collective-permute-done | bytes 245792 | tf_op jit(solution)/shard_map/ppermute | solution.py:200
  64.4 0.9 slice_add_fusion
  65.4 1.9 %collective-permute-start.6 = (f32[3,32,128]{2,1,0:T(8,128)S(1)}, f32[3,32,128]{2,1,0:T(8,128)S(1)}, u32[]{:S(2)}, u32[]{:S(2)}) collective-permute-start(f32[3,32,128]{2,1,0:T(8,128)S(1)} %get-tuple-element.26.high_ref), channel_id=1, source_target_pairs={{0,1},{1,2},{2,3},{3,4},{4,5},{5,6},{6,7},{7,8},{8,9},{9,10},{10,1... | collective-permute-start | bytes 147464 | tf_op jit(solution)/shard_map/ppermute | solution.py:134
  67.3 9.4 %collective-permute-start.7 = (f32[3,32,128]{2,1,0:T(8,128)S(1)}, f32[3,32,128]{2,1,0:T(8,128)S(1)}, u32[]{:S(2)}, u32[]{:S(2)}) collective-permute-start(f32[3,32,128]{2,1,0:T(8,128)S(1)} %get-tuple-element.27.low_ref), channel_id=1, source_target_pairs={{1,0},{2,1},{3,2},{4,3},{5,4},{6,5},{7,6},{8,7},{9,8},{10,9},{11,1... | collective-permute-start | bytes 147464 | tf_op jit(solution)/shard_map/ppermute | solution.py:134
  76.7 7.8 %shard_map.90.part_ref = f32[6,32,128]{2,1,0:T(8,128)} custom-call(f32[3,160,128]{2,1,0:T(8,128)} %get-tuple-element.22.total_ref, f32[3,160,128]{2,1,0:T(8,128)} %copy-done.2, f32[4,128,128]{2,1,0:T(8,128)} %get-tuple-element.18.vf_ref, s32[2,32,128]{2,1,0:T(8,128)} %pairs_ref.11), custom_call_target="tpu_custom_call" | custom-call | tf_op jit(solution)/shard_map/pallas_call | solution.py:20
  84.5 0.6 copy-done.7
  85.2 8.6 %shard_map.91 = (f32[3,32,128]{2,1,0:T(8,128)}, f32[3,160,128]{2,1,0:T(8,128)}) custom-call(f32[6,32,128]{2,1,0:T(8,128)} %shard_map.90.part_ref, f32[3,32,128]{2,1,0:T(8,128)} %copy-done.4, f32[3,32,128]{2,1,0:T(8,128)} %copy-done.3, f32[3,32,128]{2,1,0:T(8,128)} %copy-done.7, f32[3,32,128]{2,1,0:T(8,128)} %copy-done.9, ...), custom_call_target="tpu_custom_call" | custom-call | tf_op jit(solution)/shard_map/pallas_call | solution.py:20
  93.8 1.9 %collective-permute-start.8 = (f32[3,160,128]{2,1,0:T(8,128)}, f32[3,160,128]{2,1,0:T(8,128)S(1)}, u32[]{:S(2)}, u32[]{:S(2)}) collective-permute-start(f32[3,160,128]{2,1,0:T(8,128)} %get-tuple-element.24.total_ref), channel_id=1, source_target_pairs={{0,256},{256,0},{1,257},{257,1},{2,258},{258,2},{3,259},{259,3},{4... | collective-permute-start | bytes 737288 | tf_op jit(solution)/shard_map/ppermute | solution.py:258
  95.7 0.8 fusion
  96.5 0.9 collective-permute-done.8.other_ref
  97.4 3.5 %collective-permute-start.10 = (f32[3,16,128]{2,1,0:T(8,128)S(1)}, f32[3,16,128]{2,1,0:T(8,128)S(1)}, u32[]{:S(2)}, u32[]{:S(2)}) collective-permute-start(f32[3,16,128]{2,1,0:T(8,128)S(1)} %slice_add_fusion.4), channel_id=1, source_target_pairs={{1,0},{2,1},{3,2},{4,3},{5,4},{6,5},{7,6},{8,7},{9,8},{10,9},{11,1... | collective-permute-start | bytes 73736 | tf_op jit(solution)/shard_map/ppermute | solution.py:134
  100.9 2.3 %collective-permute-start.9 = (f32[3,16,128]{2,1,0:T(8,128)S(1)}, f32[3,16,128]{2,1,0:T(8,128)S(1)}, u32[]{:S(2)}, u32[]{:S(2)}) collective-permute-start(f32[3,16,128]{2,1,0:T(8,128)S(1)} %slice_add_fusion.5), channel_id=1, source_target_pairs={{0,1},{1,2},{2,3},{3,4},{4,5},{5,6},{6,7},{7,8},{8,9},{9,10},{10,1... | collective-permute-start | bytes 73736 | tf_op jit(solution)/shard_map/ppermute | solution.py:134
  103.3 8.8 %collective-permute-done.9.prev_ref = f32[3,16,128]{2,1,0:T(8,128)S(1)} collective-permute-done((f32[3,16,128]{2,1,0:T(8,128)S(1)}, f32[3,16,128]{2,1,0:T(8,128)S(1)}, u32[]{:S(2)}, u32[]{:S(2)}) %collective-permute-start.9) | collective-permute-done | bytes 24608 | tf_op jit(solution)/shard_map/ppermute | solution.py:134
  112.1 0.6 copy-done.14
  112.7 2.0 %shard_map.92 = f32[3,16384]{1,0:T(4,128)} custom-call(f32[3,160,128]{2,1,0:T(8,128)} %get-tuple-element.24.total_ref, f32[3,160,128]{2,1,0:T(8,128)} %copy-done, f32[3,16,128]{2,1,0:T(8,128)} %copy-done.14, f32[3,16,128]{2,1,0:T(8,128)} %copy-done.13, f32[4,128,128]{2,1,0:T(8,128)} %get-tuple-element.18.vf_ref), custom_call_target="tpu_custom_call" | custom-call | tf_op jit(solution)/shard_map/pallas_call | solution.py:20
  (34 shorter events, 0.1 us)
Async XLA Ops:
  1.5 19.6 %collective-permute-start.1 = (f32[4,2048]{1,0:T(4,128)S(1)}, f32[4,2048]{1,0:T(4,128)S(1)}, u32[]{:S(2)}, u32[]{:S(2)}) collective-permute-start(f32[4,2048]{1,0:T(4,128)S(1)} %get-tuple-element.30), channel_id=1, source_target_pairs={{1,0},{2,1},{3,2},{4,3},{5,4},{6,5},{7,6},{8,7},{9,8},{10,9},{11,1... | collective-permute-start | bytes 98312 | tf_op jit(solution)/shard_map/ppermute | solution.py:134
  8.1 13.0 %collective-permute-start = (f32[4,2048]{1,0:T(4,128)S(1)}, f32[4,2048]{1,0:T(4,128)S(1)}, u32[]{:S(2)}, u32[]{:S(2)}) collective-permute-start(f32[4,2048]{1,0:T(4,128)S(1)} %get-tuple-element.31), channel_id=1, source_target_pairs={{0,1},{1,2},{2,3},{3,4},{4,5},{5,6},{6,7},{7,8},{8,9},{9,10},{10,1... | collective-permute-start | bytes 98312 | tf_op jit(solution)/shard_map/ppermute | solution.py:134
  21.1 0.6 copy-start.11
  21.1 0.6 copy-start.12
  27.9 3.6 %collective-permute-start.2 = (f32[3,160,128]{2,1,0:T(8,128)}, f32[3,160,128]{2,1,0:T(8,128)S(1)}, u32[]{:S(2)}, u32[]{:S(2)}) collective-permute-start(f32[3,160,128]{2,1,0:T(8,128)} %get-tuple-element.17.total_ref), channel_id=1, source_target_pairs={{0,256},{256,0},{1,257},{257,1},{2,258},{258,2},{3,259},{259,3},{4... | collective-permute-start | bytes 737288 | tf_op jit(solution)/shard_map/ppermute | solution.py:200
  31.5 12.2 %copy-start.1 = (f32[3,160,128]{2,1,0:T(8,128)}, f32[3,160,128]{2,1,0:T(8,128)S(1)}, u32[]{:S(2)}) copy-start(f32[3,160,128]{2,1,0:T(8,128)S(1)} %collective-permute-done.2.other_ref) | copy-start | bytes 737284
  32.4 19.2 %copy-start.5 = (f32[3,32,128]{2,1,0:T(8,128)}, f32[3,32,128]{2,1,0:T(8,128)S(1)}, u32[]{:S(2)}) copy-start(f32[3,32,128]{2,1,0:T(8,128)S(1)} %get-tuple-element.28.high_ref) | copy-start | bytes 147460
  32.4 19.2 %copy-start.6 = (f32[3,32,128]{2,1,0:T(8,128)}, f32[3,32,128]{2,1,0:T(8,128)S(1)}, u32[]{:S(2)}) copy-start(f32[3,32,128]{2,1,0:T(8,128)S(1)} %get-tuple-element.29.low_ref) | copy-start | bytes 147460
  32.4 19.2 %collective-permute-start.3 = (f32[3,32,128]{2,1,0:T(8,128)S(1)}, f32[3,32,128]{2,1,0:T(8,128)S(1)}, u32[]{:S(2)}, u32[]{:S(2)}) collective-permute-start(f32[3,32,128]{2,1,0:T(8,128)S(1)} %get-tuple-element.28.high_ref), channel_id=1, source_target_pairs={{0,1},{1,2},{2,3},{3,4},{4,5},{5,6},{6,7},{7,8},{8,9},{9,10},{10,1... | collective-permute-start | bytes 147464 | tf_op jit(solution)/shard_map/ppermute | solution.py:134
  34.3 17.2 %collective-permute-start.4 = (f32[3,32,128]{2,1,0:T(8,128)S(1)}, f32[3,32,128]{2,1,0:T(8,128)S(1)}, u32[]{:S(2)}, u32[]{:S(2)}) collective-permute-start(f32[3,32,128]{2,1,0:T(8,128)S(1)} %get-tuple-element.29.low_ref), channel_id=1, source_target_pairs={{1,0},{2,1},{3,2},{4,3},{5,4},{6,5},{7,6},{8,7},{9,8},{10,9},{11,1... | collective-permute-start | bytes 147464 | tf_op jit(solution)/shard_map/ppermute | solution.py:134
  51.6 0.6 copy-start.8
  51.6 0.6 copy-start.10
  60.8 3.6 %collective-permute-start.5 = (f32[3,160,128]{2,1,0:T(8,128)}, f32[3,160,128]{2,1,0:T(8,128)S(1)}, u32[]{:S(2)}, u32[]{:S(2)}) collective-permute-start(f32[3,160,128]{2,1,0:T(8,128)} %get-tuple-element.22.total_ref), channel_id=1, source_target_pairs={{0,256},{256,0},{1,257},{257,1},{2,258},{258,2},{3,259},{259,3},{4... | collective-permute-start | bytes 737288 | tf_op jit(solution)/shard_map/ppermute | solution.py:200
  64.4 12.2 %copy-start.2 = (f32[3,160,128]{2,1,0:T(8,128)}, f32[3,160,128]{2,1,0:T(8,128)S(1)}, u32[]{:S(2)}) copy-start(f32[3,160,128]{2,1,0:T(8,128)S(1)} %collective-permute-done.5.other_ref) | copy-start | bytes 737284
  65.3 19.2 %copy-start.3 = (f32[3,32,128]{2,1,0:T(8,128)}, f32[3,32,128]{2,1,0:T(8,128)S(1)}, u32[]{:S(2)}) copy-start(f32[3,32,128]{2,1,0:T(8,128)S(1)} %get-tuple-element.26.high_ref) | copy-start | bytes 147460
  65.4 19.2 %copy-start.4 = (f32[3,32,128]{2,1,0:T(8,128)}, f32[3,32,128]{2,1,0:T(8,128)S(1)}, u32[]{:S(2)}) copy-start(f32[3,32,128]{2,1,0:T(8,128)S(1)} %get-tuple-element.27.low_ref) | copy-start | bytes 147460
  65.4 19.2 %collective-permute-start.6 = (f32[3,32,128]{2,1,0:T(8,128)S(1)}, f32[3,32,128]{2,1,0:T(8,128)S(1)}, u32[]{:S(2)}, u32[]{:S(2)}) collective-permute-start(f32[3,32,128]{2,1,0:T(8,128)S(1)} %get-tuple-element.26.high_ref), channel_id=1, source_target_pairs={{0,1},{1,2},{2,3},{3,4},{4,5},{5,6},{6,7},{7,8},{8,9},{9,10},{10,1... | collective-permute-start | bytes 147464 | tf_op jit(solution)/shard_map/ppermute | solution.py:134
  67.3 17.2 %collective-permute-start.7 = (f32[3,32,128]{2,1,0:T(8,128)S(1)}, f32[3,32,128]{2,1,0:T(8,128)S(1)}, u32[]{:S(2)}, u32[]{:S(2)}) collective-permute-start(f32[3,32,128]{2,1,0:T(8,128)S(1)} %get-tuple-element.27.low_ref), channel_id=1, source_target_pairs={{1,0},{2,1},{3,2},{4,3},{5,4},{6,5},{7,6},{8,7},{9,8},{10,9},{11,1... | collective-permute-start | bytes 147464 | tf_op jit(solution)/shard_map/ppermute | solution.py:134
  84.5 0.6 copy-start.7
  84.5 0.6 copy-start.9
  93.8 3.6 %collective-permute-start.8 = (f32[3,160,128]{2,1,0:T(8,128)}, f32[3,160,128]{2,1,0:T(8,128)S(1)}, u32[]{:S(2)}, u32[]{:S(2)}) collective-permute-start(f32[3,160,128]{2,1,0:T(8,128)} %get-tuple-element.24.total_ref), channel_id=1, source_target_pairs={{0,256},{256,0},{1,257},{257,1},{2,258},{258,2},{3,259},{259,3},{4... | collective-permute-start | bytes 737288 | tf_op jit(solution)/shard_map/ppermute | solution.py:258
  97.4 14.7 %copy-start = (f32[3,160,128]{2,1,0:T(8,128)}, f32[3,160,128]{2,1,0:T(8,128)S(1)}, u32[]{:S(2)}) copy-start(f32[3,160,128]{2,1,0:T(8,128)S(1)} %collective-permute-done.8.other_ref) | copy-start | bytes 737284
  97.4 5.9 %collective-permute-start.10 = (f32[3,16,128]{2,1,0:T(8,128)S(1)}, f32[3,16,128]{2,1,0:T(8,128)S(1)}, u32[]{:S(2)}, u32[]{:S(2)}) collective-permute-start(f32[3,16,128]{2,1,0:T(8,128)S(1)} %slice_add_fusion.4), channel_id=1, source_target_pairs={{1,0},{2,1},{3,2},{4,3},{5,4},{6,5},{7,6},{8,7},{9,8},{10,9},{11,1... | collective-permute-start | bytes 73736 | tf_op jit(solution)/shard_map/ppermute | solution.py:134
  100.9 11.2 %collective-permute-start.9 = (f32[3,16,128]{2,1,0:T(8,128)S(1)}, f32[3,16,128]{2,1,0:T(8,128)S(1)}, u32[]{:S(2)}, u32[]{:S(2)}) collective-permute-start(f32[3,16,128]{2,1,0:T(8,128)S(1)} %slice_add_fusion.5), channel_id=1, source_target_pairs={{0,1},{1,2},{2,3},{3,4},{4,5},{5,6},{6,7},{7,8},{8,9},{9,10},{10,1... | collective-permute-start | bytes 73736 | tf_op jit(solution)/shard_map/ppermute | solution.py:134
  103.3 8.8 %copy-start.13 = (f32[3,16,128]{2,1,0:T(8,128)}, f32[3,16,128]{2,1,0:T(8,128)S(1)}, u32[]{:S(2)}) copy-start(f32[3,16,128]{2,1,0:T(8,128)S(1)} %collective-permute-done.10.next_ref) | copy-start | bytes 73732
  112.1 0.6 copy-start.14

commit v2 on v1

v2 whole, which is shorter than its diff:
```python
import jax
import jax.numpy as jnp
from jax import lax
from jax.experimental import pallas as pl
from jax.experimental.pallas import tpu as pltpu
from jax.sharding import PartitionSpec as P

RIM = 2048
ITERS = 3
LANES = 128
relax_factor = 0.6
tangent_floor = 0.05

f32 = jnp.float32
bf16 = jnp.bfloat16
VM = pl.BlockSpec(memory_space=pltpu.VMEM)
SM = pl.BlockSpec(memory_space=pltpu.SMEM)
HB = pl.BlockSpec(memory_space=pltpu.HBM)


def call(body, out_shapes, *args, specs=None, scratch=(), onchip=None):
    specs = [VM] * len(args) if specs is None else specs
    args = [x if s is SM else pltpu.with_memory_space_constraint(x, pltpu.HBM if s is HB else pltpu.VMEM) for x, s in zip(args, specs)]
    shapes = [s if isinstance(s, tuple) and len(s) == 2 and isinstance(s[0], tuple) else (s, f32) for s in out_shapes]
    keep = [True] * len(shapes) if onchip is None else onchip
    return pl.pallas_call(
        body,
        out_shape=[pltpu.VMEM(s, t) if k else jax.ShapeDtypeStruct(s, t) for (s, t), k in zip(shapes, keep)],
        in_specs=specs,
        out_specs=[VM] * len(shapes),
        scratch_shapes=list(scratch),
        compiler_params=pltpu.CompilerParams(vmem_limit_bytes=24 << 20),
    )(*args)


def split(positions):
    return lax.shift_right_logical(positions, 7), positions & (LANES - 1)


def lane_gather(row, lo):
    dims = lax.GatherDimensionNumbers(
        offset_dims=(), collapsed_slice_dims=(1,), start_index_map=(1,),
        operand_batching_dims=(0,), start_indices_batching_dims=(0,),
    )
    return lax.gather(row, lo[:, :, None], dims, (1, 1), mode=lax.GatherScatterMode.PROMISE_IN_BOUNDS)


def gather_rows(table, comps, start, rows, base, his, los, sums):
    sums = [list(s) for s in sums]
    for r in range(start, start + rows):
        hits = [hi == base + r for hi in his]
        for c in range(comps):
            row = jnp.broadcast_to(table[c, r : r + 1, :], los[0].shape)
            for k, lo in enumerate(los):
                sums[k][c] = jnp.where(hits[k], lane_gather(row, lo), sums[k][c])
    return sums


def update(lam, rel, trig, scaled, bias, friction, active):
    sp, cp, sq, cq = trig
    n = (sp * cq, sp * sq, cp)
    a = (cp * cq, cp * sq, -sp)
    b = (-sq, cq)
    un = (n[0] * rel[0] + n[1] * rel[1] + n[2] * rel[2]) + bias
    ua = a[0] * rel[0] + a[1] * rel[1] + a[2] * rel[2]
    ub = b[0] * rel[0] + b[1] * rel[1]
    yn = lam[0] - scaled * un
    ya = lam[1] - scaled * ua
    yb = lam[2] - scaled * ub
    top = jnp.maximum(yn, 0.0)
    size = jnp.sqrt(ya * ya + yb * yb)
    factor = jnp.minimum(1.0, friction * top / jnp.maximum(size, tangent_floor))
    fn = active * top
    fa = active * (factor * ya)
    fb = active * (factor * yb)
    force = (
        n[0] * fn + a[0] * fa + b[0] * fb,
        n[1] * fn + a[1] * fa + b[1] * fb,
        n[2] * fn + a[2] * fa,
    )
    return (fn, fa, fb), force


def wide(ref, b, n):
    return jnp.broadcast_to(ref[pl.ds(b, 1), :], (n, LANES)).astype(bf16)


def spots(pos, half):
    hi, lo = split(pos)
    upper = (hi >= half).astype(jnp.int32)
    return (hi - half * upper).astype(f32), (lo + LANES * upper).astype(f32)


def build_columns(first, count, cols, rhs):
    ids = lax.broadcasted_iota(jnp.int32, (2 * LANES, LANES), 0).astype(f32).astype(bf16)
    zero = jnp.zeros((), bf16)
    for i in range(count):
        for side in range(2):
            sign = jnp.full((), 1 - 2 * side, bf16)
            at = pl.multiple_of((2 * (first + i) + side) * LANES, LANES)
            rhs[:, pl.ds(at, LANES)] = jnp.where(wide(cols.at[side], first + i, 2 * LANES) == ids, sign, zero)


def scatter_group(first, count, force, stage, rowsel, rhs, lhs, half):
    for c in range(3):
        high = force[c].astype(bf16).astype(f32)
        stage[2 * c, first : first + count] = high
        stage[2 * c + 1, first : first + count] = force[c] - high
    ids = lax.broadcasted_iota(jnp.int32, (half, LANES), 0).astype(f32).astype(bf16)
    zero = jnp.zeros((), bf16)
    for b in range(first, first + count):
        vals = [wide(stage.at[k], b, half) for k in range(6)]
        for side in range(2):
            at = (2 * b + side) * LANES
            hit = wide(rowsel.at[side], b, half) == ids
            for k in range(6):
                lhs[k * half : (k + 1) * half, at : at + LANES] = jnp.where(hit, vals[k], zero)
    deep = slice(2 * first * LANES, 2 * (first + count) * LANES)
    return lax.dot_general(lhs[:, deep], rhs[:, deep], (((1,), (1,)), ((), ())), preferred_element_type=f32)


def write_total(prod, total, half):
    for c in range(3):
        both = prod[2 * c * half : (2 * c + 1) * half] + prod[(2 * c + 1) * half : (2 * c + 2) * half]
        total[c, :half, :] = both[:, :LANES]
        total[c, half:, :] = both[:, LANES:]


def on_device(v_free, inv_mass, pairs, angles, bias, friction, counts):
    width = v_free.shape[1]
    own = width // LANES
    rim = RIM // LANES
    rows = own + 2 * rim
    half = rows // 2
    blocks = bias.shape[0]
    slots = (blocks, LANES)
    deep = 2 * blocks * LANES
    group = 8
    count = lax.axis_size("grp")
    core = lax.axis_index("cell").astype(jnp.int32).reshape(1)
    steps = [(i, i + 1) for i in range(count - 1)] + [(count + i + 1, count + i) for i in range(count - 1)]

    def around(mine):
        return lax.all_gather(lax.ppermute(mine, ("cell", "grp"), steps), "cell")

    def load(v_hbm, mass_hbm, counts_hbm, pairs_hbm, angles_hbm, bias_hbm, fric_hbm, core_ref,
             vf, mine, act, pairs_ref, angles_ref, bias_ref, fric_ref, v_ref, counts_ref, sems):
        pairs_of = [(v_hbm, v_ref), (mass_hbm, vf.at[3]), (counts_hbm, counts_ref), (pairs_hbm, pairs_ref), (angles_hbm, angles_ref),
                    (bias_hbm, bias_ref), (fric_hbm, fric_ref)]
        copies = [pltpu.make_async_copy(src, dst, sems.at[i]) for i, (src, dst) in enumerate(pairs_of)]
        for copy in copies:
            copy.start()
        copies[0].wait()
        for r in range(own):
            for c in range(3):
                vf[c, r : r + 1, :] = v_ref[c : c + 1, r * LANES : (r + 1) * LANES]
        copies[1].wait()
        upward = core_ref[0] == 0
        for c in range(4):
            mine[c] = jnp.where(upward, vf[c, own - rim :], vf[c, :rim])
        copies[2].wait()
        lane = lax.broadcasted_iota(jnp.int32, (1, LANES), 1)
        for b in range(blocks):
            act[b : b + 1, :] = jnp.where(lane < counts_ref[b], 1.0, 0.0)
        for copy in copies[3:]:
            copy.wait()

    vf, mine, act, pairs, angles, bias, friction = call(
        load,
        [(4, own, LANES), (4, rim, LANES), slots, (pairs.shape, jnp.int32), angles.shape, slots, slots],
        v_free, inv_mass.reshape(own, LANES), counts, pairs, angles, bias, friction, core,
        specs=[HB] * 7 + [SM],
        scratch=[pltpu.VMEM((3, width), f32), pltpu.SMEM((blocks,), jnp.int32), pltpu.SemaphoreType.DMA((7,))],
    )
    got_rims = around(mine)

    def prepare(vf, pairs_ref, angles_ref, part, trig, rowsel, rhs, cols):
        for i in range(2):
            rowsel[i], cols[i] = spots(pairs_ref[i], half)
        zero = jnp.zeros((group, LANES), f32)

        def some(k, carry):
            first = pl.multiple_of(k * group, group)
            at = pl.ds(first, group)
            build_columns(first, group, cols, rhs)
            for i in range(2):
                trig[2 * i, at, :] = jnp.sin(angles_ref[i, at, :])
                trig[2 * i + 1, at, :] = jnp.cos(angles_ref[i, at, :])
            his, los = zip(*(split(pairs_ref[i, at, :]) for i in range(2)))
            one, two = gather_rows(vf, 4, 0, own, rim, his, los, [[zero] * 4, [zero] * 4])
            for c in range(4):
                part[c, at, :] = one[c]
                part[4 + c, at, :] = two[c]
            return carry

        lax.fori_loop(0, blocks // group, some, 0)

    part, trig, rowsel, rhs = call(
        prepare,
        [(8,) + slots, (4,) + slots, (2,) + slots, ((2 * LANES, deep), bf16)],
        vf, pairs, angles,
        scratch=[pltpu.VMEM((2,) + slots, f32)],
    )

    def first_sweep(part_ref, got_ref, pairs_ref, trig_ref, act_ref, bias_ref, fric_ref, rowsel_ref, rhs_ref,
                    rims, scaled_ref, lam_ref, total, lhs, stage):
        for c in range(4):
            rims[c, :rim] = got_ref[0, c]
            rims[c, rim:] = got_ref[1, c]
        zero = jnp.zeros((group, LANES), f32)
        prod = None
        for k in range(blocks // group):
            at = slice(group * k, group * (k + 1))
            hi, lo = split(pairs_ref[1, at, :])
            two = [[part_ref[4 + c, at, :] for c in range(4)]]
            two = gather_rows(rims, 4, 0, rim, 0, [hi], [lo], two)
            (two,) = gather_rows(rims, 4, rim, rim, own, [hi], [lo], two)
            rel = [part_ref[c, at, :] - two[c] for c in range(3)]
            scaled = relax_factor * (1.0 / (part_ref[3, at, :] + two[3]))
            scaled_ref[at, :] = scaled
            fresh, force = update(
                (zero, zero, zero), rel, [trig_ref[i, at, :] for i in range(4)],
                scaled, bias_ref[at, :], fric_ref[at, :], act_ref[at, :],
            )
            for c in range(3):
                lam_ref[c, at, :] = fresh[c]
            more = scatter_group(group * k, group, force, stage, rowsel_ref, rhs_ref, lhs, half)
            prod = more if prod is None else prod + more
        write_total(prod, total, half)

    scatter_scratch = [pltpu.VMEM((6 * half, deep), bf16), pltpu.VMEM((6,) + slots, f32)]
    rims, scaled, lam, total = call(
        first_sweep,
        [(4, 2 * rim, LANES), slots, (3,) + slots, (3, rows, LANES)],
        part, got_rims, pairs, trig, act, bias, friction, rowsel, rhs,
        scratch=scatter_scratch,
    )

    def edges(wide_rows):
        def body(both_ref, core_ref, mine, *kept):
            upward = core_ref[0] == 0
            for c in range(3):
                below = both_ref[0, c, :wide_rows] + both_ref[1, c, :wide_rows]
                above = both_ref[0, c, rows - wide_rows :] + both_ref[1, c, rows - wide_rows :]
                mine[c] = jnp.where(upward, above, below)
                if kept:
                    kept[0][c] = below
                    kept[1][c] = above

        return body

    for sweep in range(1, ITERS):
        both = lax.all_gather(total, "cell")
        mine, low, high = call(edges(2 * rim), [(3, 2 * rim, LANES)] * 3, both, core, specs=[VM, SM])
        got = around(mine)

        def inner(both_ref, vf_ref, pairs_ref, part, vel):
            for c in range(3):
                vel[c] = vf_ref[c, rim : own - rim] + vf_ref[3, rim : own - rim] * (
                    both_ref[0, c, 2 * rim : own] + both_ref[1, c, 2 * rim : own]
                )
            zero = jnp.zeros((group, LANES), f32)

            def some(k, carry):
                at = pl.ds(pl.multiple_of(k * group, group), group)
                his, los = zip(*(split(pairs_ref[i, at, :]) for i in range(2)))
                one, two = gather_rows(vel, 3, 0, own - 2 * rim, 2 * rim, his, los, [[zero] * 3, [zero] * 3])
                for c in range(3):
                    part[c, at, :] = one[c]
                    part[3 + c, at, :] = two[c]
                return carry

            lax.fori_loop(0, blocks // group, some, 0)

        (part,) = call(
            inner, [(6,) + slots], both, vf, pairs,
            scratch=[pltpu.VMEM((3, own - 2 * rim, LANES), f32)],
        )

        def outer(part_ref, low_ref, high_ref, got_ref, vf_ref, rims_ref, pairs_ref, trig_ref, act_ref,
                  bias_ref, fric_ref, scaled_ref, old_ref, rowsel_ref, rhs_ref, lam_ref, total, vel, lhs, stage):
            for c in range(3):
                lows = low_ref[c] + got_ref[0, c]
                highs = high_ref[c] + got_ref[1, c]
                vel[c, :rim] = rims_ref[c, :rim] + rims_ref[3, :rim] * lows[:rim]
                vel[c, rim : 2 * rim] = vf_ref[c, :rim] + vf_ref[3, :rim] * lows[rim:]
                vel[c, 2 * rim : 3 * rim] = vf_ref[c, own - rim :] + vf_ref[3, own - rim :] * highs[:rim]
                vel[c, 3 * rim :] = rims_ref[c, rim:] + rims_ref[3, rim:] * highs[rim:]
            prod = None
            for k in range(blocks // group):
                at = slice(group * k, group * (k + 1))
                sums = [[part_ref[c, at, :] for c in range(3)], [part_ref[3 + c, at, :] for c in range(3)]]
                his, los = zip(*(split(pairs_ref[i, at, :]) for i in range(2)))
                skip = own - 2 * rim
                sums = gather_rows(vel, 3, rim, rim, 0, his, los, sums)
                sums = gather_rows(vel, 3, 2 * rim, rim, skip, his, los, sums)
                one, two = sums
                (two,) = gather_rows(vel, 3, 0, rim, 0, his[1:], los[1:], [two])
                (two,) = gather_rows(vel, 3, 3 * rim, rim, skip, his[1:], los[1:], [two])
                rel = [one[c] - two[c] for c in range(3)]
                fresh, force = update(
                    [old_ref[c, at, :] for c in range(3)], rel, [trig_ref[i, at, :] for i in range(4)],
                    scaled_ref[at, :], bias_ref[at, :], fric_ref[at, :], act_ref[at, :],
                )
                for c in range(3):
                    lam_ref[c, at, :] = fresh[c]
                more = scatter_group(group * k, group, force, stage, rowsel_ref, rhs_ref, lhs, half)
                prod = more if prod is None else prod + more
            write_total(prod, total, half)

        lam, total = call(
            outer,
            [(3,) + slots, (3, rows, LANES)],
            part, low, high, got, vf, rims, pairs, trig, act, bias, friction, scaled, lam, rowsel, rhs,
            scratch=[pltpu.VMEM((3, 4 * rim, LANES), f32)] + scatter_scratch,
            onchip=[sweep < ITERS - 1, True],
        )

    both = lax.all_gather(total, "cell")
    (mine,) = call(edges(rim), [(3, rim, LANES)], both, core, specs=[VM, SM])
    got = around(mine)

    def finish(both_ref, got_ref, vf_ref, out):
        for c in range(3):
            t = both_ref[0, c, rim : rim + own] + both_ref[1, c, rim : rim + own]
            head = t[:rim] + got_ref[0, c]
            tail = t[own - rim :] + got_ref[1, c]
            v = vf_ref[c] + vf_ref[3] * jnp.concatenate([head, t[rim : own - rim], tail], axis=0)
            for r in range(own):
                out[c : c + 1, r * LANES : (r + 1) * LANES] = v[r : r + 1]

    (velocity,) = call(finish, [(3, width)], both, got, vf, onchip=[False])
    return (velocity, lam)


def solution(mesh):
    return jax.shard_map(
        on_device,
        mesh=mesh,
        in_specs=(
            P(None, "grp"),
            P("grp"),
            P(None, ("cell", "grp"), None),
            P(None, ("cell", "grp"), None),
            P(("cell", "grp"), None),
            P(("cell", "grp"), None),
            P(("cell", "grp")),
        ),
        out_specs=(P(None, "grp"), P(None, ("cell", "grp"), None)),
        check_vma=False,
    )
```

time: 116 us -> 73.7 us (0.64)
  starting transfers between devices: 42.7 us -> 9.16 us
  Pallas kernels: 52.1 us -> 24.3 us
  blocking collectives: 0 us -> 14.3 us
  waiting for transfers between devices: 13 us -> 24.5 us
  local copies, waits for them, and re-layouts: 3.32 us -> 0 us
  other arithmetic: 2.68 us -> 0 us
    ppermute x11 -> x4, starting transfers between devices: 42.7 us -> 9.16 us  [around(): return lax.all_gather(lax.ppermute(mine, ('cell', 'grp'), steps), 'cell')]
    pallas_call x7 -> x11, Pallas kernels: 52.1 us -> 24.3 us  [call(): pl.pallas_call(body, out_shape=[pltpu.VMEM(s, t) if k else jax.ShapeDtype...]
    all_gather x0 -> x7, blocking collectives: none -> 14.3 us  [the longest x4 7.88 us: around(): return lax.all_gather(lax.ppermute(mine, ('cell', 'grp'), steps), 'cell')]
    ppermute x11 -> x4, waiting for transfers between devices: 13 us -> 24.5 us  [around(): return lax.all_gather(lax.ppermute(mine, ('cell', 'grp'), steps), 'cell')]
    unnamed x30 -> x0, local copies, waits for them, and re-layouts: 2.47 us -> none
    add x4 -> x0, other arithmetic: 1.83 us -> none  [the longest x2 1.82 us: on_device(): edge_high = total[:, own:] + other[:, own:]]
  transfers between devices with their start and end apart: 11 -> 4, of which waited for: 4 -> 4; matrix products, arithmetic and copies ran while one was open for 1% -> 0% of each run, Pallas kernels for 23% -> 16%
where the time goes in v2:
time: 73.7 us; the launch traced here: 73.1 us
  waiting for transfers between devices  24.5 us (33%)
  Pallas kernels  24.3 us (33%)
  blocking collectives  14.3 us (19%)
  starting transfers between devices  9.16 us (12%)
    ppermute x4, waiting for transfers between devices, around(): return lax.all_gather(lax.ppermute(mine, ('cell', 'grp'), steps), 'cell')  24.5 us
    pallas_call x11, Pallas kernels, call(): pl.pallas_call(body, out_shape=[pltpu.VMEM(s, t) if k else jax.ShapeDtype...  24.3 us
    ppermute x4, starting transfers between devices, around(): return lax.all_gather(lax.ppermute(mine, ('cell', 'grp'), steps), 'cell')  9.16 us
    all_gather x4, blocking collectives, around(): return lax.all_gather(lax.ppermute(mine, ('cell', 'grp'), steps), 'cell')  7.88 us
    all_gather x3, blocking collectives, on_device(): both = lax.all_gather(total, 'cell')  6.46 us
  transfers between devices with their start and end apart: 4, of which 4 were waited for; matrix products, arithmetic and copies ran while one was open for 0% of the time, Pallas kernels for 16%

profile of v2, /device:TPU:256, one launch (start us, length us, event | category | flops | bytes accessed | tf_op | source)
XLA Modules:
  0.0 73.1 jit_solution(685158329869141850)
XLA Ops:
  0.6 1.2 %shard_map.86 = (f32[4,128,128]{2,1,0:T(8,128)S(1)}, f32[4,16,128]{2,1,0:T(8,128)S(1)}, f32[32,128]{1,0:T(8,128)S(1)}, s32[2,32,128]{2,1,0:T(8,128)S(1)}, f32[2,...) custom-call(f32[3,16384]{1,0:T(4,128)} %v_hbm.1, f32[128,128]{1,0:T(8,128)} %bitcast.19, ...), custom_call_target="tpu_custom_call" | custom-call | tf_op jit(solution)/shard_map/pallas_call | solution.py:26
  1.8 3.4 %collective-permute-start = (f32[4,16,128]{2,1,0:T(8,128)S(1)}, f32[4,16,128]{2,1,0:T(8,128)S(1)}, u32[]{:S(2)}, u32[]{:S(2)}) collective-permute-start(f32[4,16,128]{2,1,0:T(8,128)S(1)} %get-tuple-element.31), channel_id=1, source_target_pairs={{0,1},{1,2},{2,3},{3,4},{4,5},{5,6},{6,7},{7,8},{8,9},{9,10},{10,1... | collective-permute-start | bytes 98312 | tf_op jit(solution)/shard_map/ppermute | solution.py:144
  5.2 5.8 %shard_map.87 = (f32[8,32,128]{2,1,0:T(8,128)S(1)}, f32[4,32,128]{2,1,0:T(8,128)S(1)}, f32[2,32,128]{2,1,0:T(8,128)S(1)}, bf16[256,8192]{1,0:T(8,128)(2,1)S(1)}) custom-call(f32[4,128,128]{2,1,0:T(8,128)S(1)} %get-tuple-element.27.vf.vf_ref, s32[2,32,128]{2,1,0:T(8,128)S(1)} %get-tuple-element.28.pairs_ref, f32[2,32,128]{2,1,0:T(8,128)S(1)} %get-tuple-element.29.angles_ref), custom_call_target="tpu_custom_call" | custom-call | tf_op jit(solution)/shard_map/pallas_call | solution.py:26
  11.1 2.0 %collective-permute-done = f32[4,16,128]{2,1,0:T(8,128)S(1)} collective-permute-done((f32[4,16,128]{2,1,0:T(8,128)S(1)}, f32[4,16,128]{2,1,0:T(8,128)S(1)}, u32[]{:S(2)}, u32[]{:S(2)}) %collective-permute-start) | collective-permute-done | bytes 32800 | tf_op jit(solution)/shard_map/ppermute | solution.py:144
  13.1 2.3 %all-gather = f32[8,16,128]{2,1,0:T(8,128)S(1)} all-gather(f32[4,16,128]{2,1,0:T(8,128)S(1)} %collective-permute-done), channel_id=2, replica_groups=mesh['cell'=2,'grp'=256] {'cell'}, dimensions={0}, use_global_device_ids=true | all-gather | bytes 98304 | tf_op jit(solution)/shard_map/all_gather | solution.py:144
  15.4 2.9 %shard_map.88 = (f32[4,32,128]{2,1,0:T(8,128)S(1)}, f32[32,128]{1,0:T(8,128)S(1)}, f32[3,32,128]{2,1,0:T(8,128)S(1)}, f32[3,160,128]{2,1,0:T(8,128)S(1)}) custom-call(f32[8,32,128]{2,1,0:T(8,128)S(1)} %get-tuple-element.30.part_ref, f32[2,4,16,128]{3,2,1,0:T(8,128)S(1)} %bitcast.17, s32[2,32,128]{2,1,0:T(8,128)S(1)} %get-tuple-element.28.pairs_ref, ...), custom_call_target="tpu_custom_call" | custom-call | tf_op jit(solution)/shard_map/pallas_call | solution.py:26
  18.3 2.2 %all-gather.1 = f32[6,160,128]{2,1,0:T(8,128)S(1)} all-gather(f32[3,160,128]{2,1,0:T(8,128)S(1)} %get-tuple-element.38), channel_id=3, replica_groups=mesh['cell'=2,'grp'=256] {'cell'}, dimensions={0}, use_global_device_ids=true | all-gather | bytes 737280 | tf_op jit(solution)/shard_map/all_gather | solution.py:253
  20.5 1.9 %collective-permute-start.1 = (f32[3,32,128]{2,1,0:T(8,128)S(1)}, f32[3,32,128]{2,1,0:T(8,128)S(1)}, u32[]{:S(2)}, u32[]{:S(2)}) collective-permute-start(f32[3,32,128]{2,1,0:T(8,128)S(1)} %get-tuple-element.41), channel_id=1, source_target_pairs={{0,1},{1,2},{2,3},{3,4},{4,5},{5,6},{6,7},{7,8},{8,9},{9,10},{10,1... | collective-permute-start | bytes 147464 | tf_op jit(solution)/shard_map/ppermute | solution.py:144
  22.5 2.8 %shard_map.89.part_ref = f32[6,32,128]{2,1,0:T(8,128)S(1)} custom-call(f32[2,3,160,128]{3,2,1,0:T(8,128)S(1)} %bitcast.12, f32[4,128,128]{2,1,0:T(8,128)S(1)} %get-tuple-element.27.vf.vf_ref, s32[2,32,128]{2,1,0:T(8,128)S(1)} %get-tuple-element.28.pairs_ref), custom_call_target="tpu_custom_call" | custom-call | tf_op jit(solution)/shard_map/pallas_call | solution.py:26
  25.3 6.7 %collective-permute-done.1 = f32[3,32,128]{2,1,0:T(8,128)S(1)} collective-permute-done((f32[3,32,128]{2,1,0:T(8,128)S(1)}, f32[3,32,128]{2,1,0:T(8,128)S(1)}, u32[]{:S(2)}, u32[]{:S(2)}) %collective-permute-start.1) | collective-permute-done | bytes 49184 | tf_op jit(solution)/shard_map/ppermute | solution.py:144
  31.9 1.9 %all-gather.2 = f32[6,32,128]{2,1,0:T(8,128)S(1)} all-gather(f32[3,32,128]{2,1,0:T(8,128)S(1)} %collective-permute-done.1), channel_id=4, replica_groups=mesh['cell'=2,'grp'=256] {'cell'}, dimensions={0}, use_global_device_ids=true | all-gather | bytes 147456 | tf_op jit(solution)/shard_map/all_gather | solution.py:144
  33.8 3.8 %shard_map.91 = (f32[3,32,128]{2,1,0:T(8,128)S(1)}, f32[3,160,128]{2,1,0:T(8,128)S(1)}) custom-call(f32[6,32,128]{2,1,0:T(8,128)S(1)} %shard_map.89.part_ref, f32[3,32,128]{2,1,0:T(8,128)S(1)} %get-tuple-element.39.low_ref, f32[3,32,128]{2,1,0:T(8,128)S(1)} %get-tuple-element.40.high_ref, f32[2,3,32,128]{3,2,1,0:T(8,128)S(1)} %bitcast.16, ...), custom_call_target="tpu_custom_call" | custom-call | tf_op jit(solution)/shard_map/pallas_call | solution.py:26
  37.6 2.2 %all-gather.3 = f32[6,160,128]{2,1,0:T(8,128)S(1)} all-gather(f32[3,160,128]{2,1,0:T(8,128)S(1)} %get-tuple-element.45), channel_id=5, replica_groups=mesh['cell'=2,'grp'=256] {'cell'}, dimensions={0}, use_global_device_ids=true | all-gather | bytes 737280 | tf_op jit(solution)/shard_map/all_gather | solution.py:253
  39.8 1.9 %collective-permute-start.2 = (f32[3,32,128]{2,1,0:T(8,128)S(1)}, f32[3,32,128]{2,1,0:T(8,128)S(1)}, u32[]{:S(2)}, u32[]{:S(2)}) collective-permute-start(f32[3,32,128]{2,1,0:T(8,128)S(1)} %get-tuple-element.48), channel_id=1, source_target_pairs={{0,1},{1,2},{2,3},{3,4},{4,5},{5,6},{6,7},{7,8},{8,9},{9,10},{10,1... | collective-permute-start | bytes 147464 | tf_op jit(solution)/shard_map/ppermute | solution.py:144
  41.8 2.8 %shard_map.92.part_ref = f32[6,32,128]{2,1,0:T(8,128)S(1)} custom-call(f32[2,3,160,128]{3,2,1,0:T(8,128)S(1)} %bitcast.14, f32[4,128,128]{2,1,0:T(8,128)S(1)} %get-tuple-element.27.vf.vf_ref, s32[2,32,128]{2,1,0:T(8,128)S(1)} %get-tuple-element.28.pairs_ref), custom_call_target="tpu_custom_call" | custom-call | tf_op jit(solution)/shard_map/pallas_call | solution.py:26
  44.6 6.7 %collective-permute-done.2 = f32[3,32,128]{2,1,0:T(8,128)S(1)} collective-permute-done((f32[3,32,128]{2,1,0:T(8,128)S(1)}, f32[3,32,128]{2,1,0:T(8,128)S(1)}, u32[]{:S(2)}, u32[]{:S(2)}) %collective-permute-start.2) | collective-permute-done | bytes 49184 | tf_op jit(solution)/shard_map/ppermute | solution.py:144
  51.2 1.9 %all-gather.4 = f32[6,32,128]{2,1,0:T(8,128)S(1)} all-gather(f32[3,32,128]{2,1,0:T(8,128)S(1)} %collective-permute-done.2), channel_id=6, replica_groups=mesh['cell'=2,'grp'=256] {'cell'}, dimensions={0}, use_global_device_ids=true | all-gather | bytes 147456 | tf_op jit(solution)/shard_map/all_gather | solution.py:144
  53.1 4.0 %shard_map.94 = (f32[3,32,128]{2,1,0:T(8,128)}, f32[3,160,128]{2,1,0:T(8,128)S(1)}) custom-call(f32[6,32,128]{2,1,0:T(8,128)S(1)} %shard_map.92.part_ref, f32[3,32,128]{2,1,0:T(8,128)S(1)} %get-tuple-element.46.low_ref, f32[3,32,128]{2,1,0:T(8,128)S(1)} %get-tuple-element.47.high_ref, f32[2,3,32,128]{3,2,1,0:T(8,128)S(1)} %bitcast.15, ...), custom_call_target="tpu_custom_call" | custom-call | tf_op jit(solution)/shard_map/pallas_call | solution.py:26
  57.1 2.1 %all-gather.5 = f32[6,160,128]{2,1,0:T(8,128)S(1)} all-gather(f32[3,160,128]{2,1,0:T(8,128)S(1)} %get-tuple-element.50), channel_id=7, replica_groups=mesh['cell'=2,'grp'=256] {'cell'}, dimensions={0}, use_global_device_ids=true | all-gather | bytes 737280 | tf_op jit(solution)/shard_map/all_gather | solution.py:319
  59.3 1.9 %collective-permute-start.3 = (f32[3,16,128]{2,1,0:T(8,128)S(1)}, f32[3,16,128]{2,1,0:T(8,128)S(1)}, u32[]{:S(2)}, u32[]{:S(2)}) collective-permute-start(f32[3,16,128]{2,1,0:T(8,128)S(1)} %shard_map.95), channel_id=1, source_target_pairs={{0,1},{1,2},{2,3},{3,4},{4,5},{5,6},{6,7},{7,8},{8,9},{9,10},{10,1... | collective-permute-start | bytes 73736 | tf_op jit(solution)/shard_map/ppermute | solution.py:144
  61.2 9.2 %collective-permute-done.3 = f32[3,16,128]{2,1,0:T(8,128)S(1)} collective-permute-done((f32[3,16,128]{2,1,0:T(8,128)S(1)}, f32[3,16,128]{2,1,0:T(8,128)S(1)}, u32[]{:S(2)}, u32[]{:S(2)}) %collective-permute-start.3) | collective-permute-done | bytes 24608 | tf_op jit(solution)/shard_map/ppermute | solution.py:144
  70.4 1.8 %all-gather.6 = f32[6,16,128]{2,1,0:T(8,128)S(1)} all-gather(f32[3,16,128]{2,1,0:T(8,128)S(1)} %collective-permute-done.3), channel_id=8, replica_groups=mesh['cell'=2,'grp'=256] {'cell'}, dimensions={0}, use_global_device_ids=true | all-gather | bytes 73728 | tf_op jit(solution)/shard_map/all_gather | solution.py:144
  72.3 0.8 %shard_map.96 = f32[3,16384]{1,0:T(4,128)} custom-call(f32[2,3,160,128]{3,2,1,0:T(8,128)S(1)} %bitcast.10, f32[2,3,16,128]{3,2,1,0:T(8,128)S(1)} %bitcast.18, f32[4,128,128]{2,1,0:T(8,128)S(1)} %get-tuple-element.27.vf.vf_ref), custom_call_target="tpu_custom_call" | custom-call | tf_op jit(solution)/shard_map/pallas_call | solution.py:26
  (3 shorter events, 0.0 us)
Async XLA Ops:
  1.8 11.2 %collective-permute-start = (f32[4,16,128]{2,1,0:T(8,128)S(1)}, f32[4,16,128]{2,1,0:T(8,128)S(1)}, u32[]{:S(2)}, u32[]{:S(2)}) collective-permute-start(f32[4,16,128]{2,1,0:T(8,128)S(1)} %get-tuple-element.31), channel_id=1, source_target_pairs={{0,1},{1,2},{2,3},{3,4},{4,5},{5,6},{6,7},{7,8},{8,9},{9,10},{10,1... | collective-permute-start | bytes 98312 | tf_op jit(solution)/shard_map/ppermute | solution.py:144
  20.5 11.4 %collective-permute-start.1 = (f32[3,32,128]{2,1,0:T(8,128)S(1)}, f32[3,32,128]{2,1,0:T(8,128)S(1)}, u32[]{:S(2)}, u32[]{:S(2)}) collective-permute-start(f32[3,32,128]{2,1,0:T(8,128)S(1)} %get-tuple-element.41), channel_id=1, source_target_pairs={{0,1},{1,2},{2,3},{3,4},{4,5},{5,6},{6,7},{7,8},{8,9},{9,10},{10,1... | collective-permute-start | bytes 147464 | tf_op jit(solution)/shard_map/ppermute | solution.py:144
  39.8 11.4 %collective-permute-start.2 = (f32[3,32,128]{2,1,0:T(8,128)S(1)}, f32[3,32,128]{2,1,0:T(8,128)S(1)}, u32[]{:S(2)}, u32[]{:S(2)}) collective-permute-start(f32[3,32,128]{2,1,0:T(8,128)S(1)} %get-tuple-element.48), channel_id=1, source_target_pairs={{0,1},{1,2},{2,3},{3,4},{4,5},{5,6},{6,7},{7,8},{8,9},{9,10},{10,1... | collective-permute-start | bytes 147464 | tf_op jit(solution)/shard_map/ppermute | solution.py:144
  59.3 11.2 %collective-permute-start.3 = (f32[3,16,128]{2,1,0:T(8,128)S(1)}, f32[3,16,128]{2,1,0:T(8,128)S(1)}, u32[]{:S(2)}, u32[]{:S(2)}) collective-permute-start(f32[3,16,128]{2,1,0:T(8,128)S(1)} %shard_map.95), channel_id=1, source_target_pairs={{0,1},{1,2},{2,3},{3,4},{4,5},{5,6},{6,7},{7,8},{8,9},{9,10},{10,1... | collective-permute-start | bytes 73736 | tf_op jit(solution)/shard_map/ppermute | solution.py:144
